TPU v7x, 128 devices: a whole 4x4x4 slice. The times are simulated.
128 devices in a mesh: freq: 8 (over x, y_hi), trace: 16 (over y_lo, z, core).
Axes of the slice: x: 4, y: 4 (y_hi: 2, y_lo: 2; y = y_hi * 2 + y_lo), z: 4, core: 2. Of those that a mesh axis runs over, the one named last changes fastest.
Arguments:
- traces: float32 [256, 256, 2048], P(('freq', 'trace')), may hold values from -6 to 6
- source_weights: float32 [256, 256, 512], P(None, 'trace'), may hold values from -0.0625 to 0.0625
- level_weights: float32 [4, 4096, 1024], P(None, 'trace'), may hold values from -0.1875 to 0.1875
- slowness_weights: float32 [4096, 512], P('trace'), may hold values from -0.25 to 0.25
Outputs:
- radon_image: float32 [4096, 256], P(('trace', 'freq'))
All inputs are finite; a program needn't handle non-finite values.
Results may differ from a plain program's by a relative error of at most 0.00011.
Values sent between devices are 32-bit elements; how exact they have to be, the bound alone decides.
No kernel may reach another device: no remote copies, remote signals or barrier semaphores. Data moves between devices by JAX's collectives and lax.ppermute only.
A program may use at most 128 MiB of HBM per device.

v0:
```python
import functools
import math

import jax
import jax.numpy as jnp
import numpy as np
from jax import lax
from jax.experimental import pallas as pl
from jax.experimental.pallas import tpu as pltpu
from jax.sharding import PartitionSpec as P

FREQS = 1024
TAUS = 256
F32 = jnp.float32
BF16 = jnp.bfloat16
NT = (((1,), (1,)), ((), ()))
NN = (((1,), (0,)), ((), ()))


def split(x):
    high = x.astype(BF16)
    return high, (x - high.astype(F32)).astype(BF16)


def mm(a, b, dims):
    return lax.dot_general(a, b, dims, preferred_element_type=F32)


def mm3(a_pair, b_pair, dims):
    rows = a_pair[0].shape[0]
    both = mm(jnp.concatenate(a_pair, axis=0), b_pair[0], dims)
    return both[:rows] + both[rows:] + mm(a_pair[0], b_pair[1], dims)


def tau_order(freq_count):
    per = TAUS // freq_count
    columns = np.arange(TAUS)
    owner, inner = columns // per, columns % per
    return (inner // 8) * (8 * freq_count) + owner * 8 + inner % 8


def tables(samples, freq_count):
    taus = tau_order(freq_count)
    step = samples // (4 * TAUS)
    scale = 1.0 / math.sqrt(samples) / math.sqrt(FREQS)
    n = np.arange(samples)[:, None]
    gap = (step * taus[None, :] - n) % samples
    odd = gap % 2 == 1
    cot = np.where(odd, 1.0 / np.tan(np.pi * np.where(odd, gap, 1) / samples), 0.0) * scale
    cot = cot.astype(np.float32)
    high = cot.astype(jnp.bfloat16)
    low = (cot - high.astype(np.float32)).astype(jnp.bfloat16)
    pick = (gap[: samples // 4] == 0).astype(jnp.bfloat16)
    return high, low, pick, FREQS * scale, scale


def move_groups(parts, width):
    count = len(parts)
    lanes = count * width
    group = lax.broadcasted_iota(jnp.int32, parts[0].shape, 1) // width
    turned = [p if x == 0 else pltpu.roll(p, width * x, 1) for x, p in enumerate(parts)]
    result = []
    for q in range(count):
        got = turned[(-q) % count]
        for spot in range(1, count):
            got = jnp.where(group == spot, turned[(spot - q) % count], got)
        result.append(got if q == 0 else pltpu.roll(got, lanes - width * q, 1))
    return result


def trace_kernel(keep, tone, x_ref, high_ref, low_ref, pick_ref, out_ref):
    rows = x_ref.shape[1]
    x = jnp.concatenate([x_ref[0], x_ref[1]], axis=0)
    total = x[:, :128]
    for at in range(128, x.shape[1], 128):
        total = total + x[:, at : at + 128]
    odd = lax.broadcasted_iota(jnp.int32, total.shape, 1) % 2 == 1
    mean = jnp.sum(jnp.where(odd, total, 0.0), axis=1, keepdims=True) * tone
    pair = split(x)
    imag = mm3(pair, (high_ref[...], low_ref[...]), NN)
    head = pick_ref.shape[0]
    both = mm(jnp.concatenate([p[:, :head] for p in pair], axis=0), pick_ref[...], NN)
    real = (both[: 2 * rows] + both[2 * rows :]) * keep + mean
    for tile in range(TAUS // 128):
        lanes = slice(128 * tile, 128 * tile + 128)
        parts = [real[:rows, lanes], imag[:rows, lanes], real[rows:, lanes], imag[rows:, lanes]]
        for q, block in enumerate(move_groups(parts, 32)):
            out_ref[4 * tile + q] = block.reshape(out_ref.shape[1:])


def trace_blocks(traces, freq_count, trace_count):
    shots, offsets, samples = traces.shape
    box = offsets // trace_count
    steps = 4
    high, low, pick, keep, tone = tables(samples, freq_count)
    whole = lambda a: pl.BlockSpec(a.shape, lambda i: (0, 0))
    return pl.pallas_call(
        functools.partial(trace_kernel, keep, tone),
        grid=(steps,),
        in_specs=[
            pl.BlockSpec((shots, offsets // steps, samples), lambda i: (0, i, 0)),
            whole(high),
            whole(low),
            whole(pick),
        ],
        out_specs=pl.BlockSpec(
            (freq_count, trace_count // steps, box, 128), lambda i: (0, i, 0, 0)
        ),
        out_shape=jax.ShapeDtypeStruct((freq_count, trace_count, box, 128), F32),
        compiler_params=pltpu.CompilerParams(vmem_limit_bytes=32 << 20),
        name="trace_blocks",
    )(traces, jnp.asarray(high), jnp.asarray(low), jnp.asarray(pick))


def gram_kernel(values_ref, source_ref, out_ref, acc_ref):
    step = pl.program_id(0)
    depth = values_ref.shape[0] * values_ref.shape[1]
    turned = values_ref[...].reshape(depth, 128).T
    pair = split(turned)
    source = source_ref[...]
    source = source.reshape(source.shape[0] // 2, 2, *source.shape[1:])
    acc = None
    for shot in range(2):
        rows = slice(64 * shot, 64 * shot + 64)
        weights = split(source[:, shot].reshape(depth, source.shape[3]))
        term = mm3((pair[0][rows], pair[1][rows]), weights, NN)
        acc = term if acc is None else acc + term

    @pl.when(step == 0)
    def _():
        acc_ref[...] = acc

    @pl.when(step > 0)
    def _():
        acc_ref[...] += acc

    @pl.when(step == pl.num_programs(0) - 1)
    def _():
        out_ref[...] = turn(acc_ref[...])


def turn(both):
    half, width = both.shape[0] // 2, both.shape[1] // 2
    real = both[:half, :width] - both[half:, width:]
    imag = both[half:, :width] + both[:half, width:]
    return jnp.concatenate([real, imag], axis=0)


def gram(values, sources):
    senders, box, lanes = values.shape
    shots, _, width = sources.shape
    steps = 4
    return pl.pallas_call(
        gram_kernel,
        grid=(steps,),
        in_specs=[
            pl.BlockSpec((senders // steps, box, lanes), lambda i: (i, 0, 0)),
            pl.BlockSpec((shots // steps, box, width), lambda i: (i, 0, 0)),
        ],
        out_specs=pl.BlockSpec((64, width // 2), lambda i: (0, 0)),
        out_shape=jax.ShapeDtypeStruct((64, width // 2), F32),
        scratch_shapes=[pltpu.VMEM((64, width), F32)],
        compiler_params=pltpu.CompilerParams(vmem_limit_bytes=32 << 20),
        name="gram",
    )(values, sources)


def own_kernel(c_ref, w_ref, own_ref, high_ref, low_ref):
    k = c_ref.shape[1]
    weights = w_ref[0]
    own = split(jnp.concatenate([weights[:, :k], weights[:, 2 * k : 3 * k]], axis=0))
    own_ref[...] = turn(mm3(split(c_ref[...]), own, NT))
    high, low = split(jnp.concatenate([weights[:, k : 2 * k], weights[:, 3 * k :]], axis=0))
    high_ref[...] = high
    low_ref[...] = low


def own_part(c, weights, level):
    rows, k = c.shape
    return pl.pallas_call(
        own_kernel,
        grid=(1,),
        in_specs=[
            pl.BlockSpec((rows, k), lambda i: (0, 0)),
            pl.BlockSpec((1, k, 4 * k), lambda i: (level, 0, 0)),
        ],
        out_specs=[
            pl.BlockSpec((rows, k), lambda i: (0, 0)),
            pl.BlockSpec((2 * k, k), lambda i: (0, 0)),
            pl.BlockSpec((2 * k, k), lambda i: (0, 0)),
        ],
        out_shape=[
            jax.ShapeDtypeStruct((rows, k), F32),
            jax.ShapeDtypeStruct((2 * k, k), BF16),
            jax.ShapeDtypeStruct((2 * k, k), BF16),
        ],
        compiler_params=pltpu.CompilerParams(vmem_limit_bytes=16 << 20),
        cost_estimate=pl.CostEstimate(flops=10**8, bytes_accessed=10**6, transcendentals=0),
        name="own_part",
    )(c, weights)


def joined(own_ref, c_ref, high_ref, low_ref):
    return own_ref[...] + turn(mm3(split(c_ref[...]), (high_ref[...], low_ref[...]), NT))


def join_kernel(own_ref, c_ref, high_ref, low_ref, out_ref):
    out_ref[...] = joined(own_ref, c_ref, high_ref, low_ref)


def last_kernel(own_ref, c_ref, high_ref, low_ref, e_ref, out_ref):
    c = joined(own_ref, c_ref, high_ref, low_ref)
    half = c.shape[0] // 2
    row = jnp.concatenate([c[:half], -c[half:]], axis=1)
    values = mm3(split(row), split(e_ref[...]), NT)
    for tile in range(values.shape[1] // 128):
        lanes = slice(128 * tile, 128 * tile + 128)
        parts = [values[8 * g : 8 * g + 8, lanes] for g in range(4)]
        for q, block in enumerate(move_groups(parts, 32)):
            out_ref[4 * tile + q] = block


def join_part(own, c, high, low):
    return pl.pallas_call(
        join_kernel,
        out_shape=jax.ShapeDtypeStruct(c.shape, F32),
        compiler_params=pltpu.CompilerParams(vmem_limit_bytes=16 << 20),
        name="join_part",
    )(own, c, high, low)


def last_part(own, c, high, low, e, freq_count):
    return pl.pallas_call(
        last_kernel,
        out_shape=jax.ShapeDtypeStruct((freq_count, 8, 128), F32),
        compiler_params=pltpu.CompilerParams(vmem_limit_bytes=16 << 20),
        name="last_part",
    )(own, c, high, low, e)


def final_kernel(x_ref, out_ref):
    x = x_ref[...].reshape(-1, 128)
    x = jnp.concatenate([x, jnp.zeros_like(x)], axis=0).T
    low = lax.broadcasted_iota(jnp.int32, (32, 128), 1) < 64
    for tile in range(2):
        first = x[64 * tile : 64 * tile + 32]
        second = x[64 * tile + 32 : 64 * tile + 64]
        out_ref[:, 128 * tile : 128 * tile + 128] = jnp.where(
            low, first, pltpu.roll(second, 64, 1)
        )


def final_part(x):
    return pl.pallas_call(
        final_kernel,
        out_shape=jax.ShapeDtypeStruct((32, TAUS), F32),
        compiler_params=pltpu.CompilerParams(vmem_limit_bytes=16 << 20),
        name="final_part",
    )(x)


def from_partner(block, axis, apart):
    count = lax.axis_size(axis)
    return lax.ppermute(block, axis, [(at, at ^ (1 << apart)) for at in range(count)])


def body(traces, source_weights, level_weights, slowness_weights):
    freq_count = lax.axis_size("freq")
    trace_count = lax.axis_size("trace")
    blocks = trace_blocks(traces, freq_count, trace_count)
    blocks = blocks.reshape(freq_count * trace_count, *blocks.shape[2:])
    values = lax.all_to_all(blocks, ("freq", "trace"), split_axis=0, concat_axis=0, tiled=True)
    c = gram(values, source_weights)
    levels = level_weights.shape[0]
    for level in range(levels):
        partner = from_partner(c, "trace", level)
        own, high, low = own_part(c, level_weights, level)
        if level < levels - 1:
            c = join_part(own, partner, high, low)
        else:
            out = last_part(own, partner, high, low, slowness_weights, freq_count)
    out = lax.all_to_all(out, "freq", split_axis=0, concat_axis=0, tiled=True)
    return final_part(out)


def solution(mesh):
    return jax.shard_map(
        body,
        mesh=mesh,
        in_specs=(
            P(("freq", "trace"), None, None),
            P(None, "trace", None),
            P(None, "trace", None),
            P("trace", None),
        ),
        out_specs=P(("trace", "freq"), None),
        check_vma=False,
    )
```

profile of v0, /device:TPU:0, one launch (start us, length us, event | category | flops | bytes accessed | tf_op | source)
XLA Modules:
  0.0 70.9 jit_solution(12805300731708742953)
XLA Ops:
  0.0 0.0 copy-start.1
  0.0 2.3 %copy-done.2 = f32[2,256,2048]{2,1,0:T(8,128)S(1)} copy-done((f32[2,256,2048]{2,1,0:T(8,128)S(1)}, f32[2,256,2048]{2,1,0:T(8,128)}, u32[]{:S(2)}) %copy-start.2) | copy-done | bytes 4194328
  2.3 0.0 copy-start.3
  2.3 1.4 %copy-done.3 = bf16[2048,256]{1,0:T(8,128)(2,1)S(1)} copy-done((bf16[2048,256]{1,0:T(8,128)(2,1)S(1)}, bf16[2048,256]{1,0:T(8,128)(2,1)}, u32[]{:S(2)}) %copy-start.3) | copy-done | bytes 1048600
  3.8 0.0 copy-start.4
  3.8 1.4 %copy-done.4 = bf16[2048,256]{1,0:T(8,128)(2,1)S(1)} copy-done((bf16[2048,256]{1,0:T(8,128)(2,1)S(1)}, bf16[2048,256]{1,0:T(8,128)(2,1)}, u32[]{:S(2)}) %copy-start.4) | copy-done | bytes 1048600
  5.2 0.9 %copy-done.6 = bf16[512,256]{1,0:T(8,128)(2,1)S(1)} copy-done((bf16[512,256]{1,0:T(8,128)(2,1)S(1)}, bf16[512,256]{1,0:T(8,128)(2,1)}, u32[]{:S(2)}) %copy-start.6) | copy-done | bytes 262168
  6.1 3.7 %trace_blocks.1 = f32[8,16,16,128]{3,2,1,0:T(8,128)S(1)} custom-call(f32[2,256,2048]{2,1,0:T(8,128)S(1)} %copy-done.2, bf16[2048,256]{1,0:T(8,128)(2,1)S(1)} %copy-done.4, bf16[2048,256]{1,0:T(8,128)(2,1)S(1)} %copy-done.3, bf16[512,256]{1,0:T(8,128)(2,1)S(1)} %copy-done.6), custom_call_target="tpu_custom_call" | custom-call | tf_op jit(solution)/shard_map/trace_blocks/pallas_call | solution.py:97
  9.9 30.3 %all_to_all.10.values_ref = f32[128,16,128]{2,1,0:T(8,128)S(1)} all-to-all(f32[128,16,128]{2,1,0:T(8,128)S(1)} %bitcast.1), channel_id=1, replica_groups=mesh['freq'=8,'trace'=16] {'freq','trace'}, dimensions={0} | all-to-all | bytes 2097152 | tf_op jit(solution)/shard_map/all_to_all | solution.py:272
  40.2 0.0 copy-done.1
  40.2 2.2 %gram.1.c_ref = f32[64,256]{1,0:T(8,128)S(1)} custom-call(f32[128,16,128]{2,1,0:T(8,128)S(1)} %all_to_all.10.values_ref, f32[256,16,512]{2,1,0:T(8,128)S(1)} %copy-done.1), custom_call_target="tpu_custom_call" | custom-call | tf_op jit(solution)/shard_map/gram/pallas_call | solution.py:153
  42.4 0.1 collective-permute-start
  42.5 0.0 copy-done
  42.5 0.3 own_part.4
  42.8 0.9 %collective-permute-done.c_ref = f32[64,256]{1,0:T(8,128)S(1)} collective-permute-done((f32[64,256]{1,0:T(8,128)S(1)}, f32[64,256]{1,0:T(8,128)S(1)}, u32[]{:S(2)}, u32[]{:S(2)}) %collective-permute-start) | collective-permute-done | bytes 65568 | tf_op jit(solution)/shard_map/ppermute | solution.py:264
  43.7 0.3 join_part.3.c_ref
  44.0 0.3 collective-permute-start.1
  44.3 0.3 own_part.5
  44.7 3.7 %collective-permute-done.1.c_ref = f32[64,256]{1,0:T(8,128)S(1)} collective-permute-done((f32[64,256]{1,0:T(8,128)S(1)}, f32[64,256]{1,0:T(8,128)S(1)}, u32[]{:S(2)}, u32[]{:S(2)}) %collective-permute-start.1) | collective-permute-done | bytes 65568 | tf_op jit(solution)/shard_map/ppermute | solution.py:264
  48.3 0.3 join_part.4.c_ref
  48.6 0.0 copy-start.5
  48.6 0.2 collective-permute-start.2
  48.8 0.3 own_part.6
  49.1 5.3 %collective-permute-done.2.c_ref = f32[64,256]{1,0:T(8,128)S(1)} collective-permute-done((f32[64,256]{1,0:T(8,128)S(1)}, f32[64,256]{1,0:T(8,128)S(1)}, u32[]{:S(2)}, u32[]{:S(2)}) %collective-permute-start.2) | collective-permute-done | bytes 65568 | tf_op jit(solution)/shard_map/ppermute | solution.py:264
  54.5 0.3 join_part.5.c_ref
  54.8 0.6 collective-permute-start.3
  55.4 0.3 own_part.7
  55.7 3.4 %collective-permute-done.3.c_ref = f32[64,256]{1,0:T(8,128)S(1)} collective-permute-done((f32[64,256]{1,0:T(8,128)S(1)}, f32[64,256]{1,0:T(8,128)S(1)}, u32[]{:S(2)}, u32[]{:S(2)}) %collective-permute-start.3) | collective-permute-done | bytes 65568 | tf_op jit(solution)/shard_map/ppermute | solution.py:264
  59.1 0.0 copy-done.5
  59.1 0.8 %last_part.1 = f32[8,8,128]{2,1,0:T(8,128)S(1)} custom-call(f32[64,256]{1,0:T(8,128)S(1)} %get-tuple-element.26.own_ref, f32[64,256]{1,0:T(8,128)S(1)} %collective-permute-done.3.c_ref, bf16[512,256]{1,0:T(8,128)(2,1)S(1)} %get-tuple-element.27.high_ref, bf16[512,256]{1,0:T(8,128)(2,1)S(1)} %get-tuple-element.28.low_ref, f32[256,512]{1,0:T(8,128)S(1)} %copy-done.5), custom_call_target="tpu_custom_call" | custom-call | tf_op jit(solution)/shard_map/last_part/pallas_call | solution.py:233
  59.9 10.1 %all_to_all.11.x_ref = f32[8,8,128]{2,1,0:T(8,128)S(1)} all-to-all(f32[8,8,128]{2,1,0:T(8,128)S(1)} %last_part.1), channel_id=1, replica_groups=mesh['freq'=8,'trace'=16] {'freq'}, dimensions={0} | all-to-all | bytes 65536 | tf_op jit(solution)/shard_map/all_to_all | solution.py:282
  70.1 0.8 %final_part.1 = f32[32,256]{1,0:T(8,128)} custom-call(f32[8,8,128]{2,1,0:T(8,128)S(1)} %all_to_all.11.x_ref), custom_call_target="tpu_custom_call" | custom-call | tf_op jit(solution)/shard_map/final_part/pallas_call | solution.py:254
  (3 shorter events, 0.0 us)
Async XLA Ops:
  0.0 40.2 %copy-start.1 = (f32[256,16,512]{2,1,0:T(8,128)S(1)}, f32[256,16,512]{2,1,0:T(8,128)}, u32[]{:S(2)}) copy-start(f32[256,16,512]{2,1,0:T(8,128)} %source_ref.1) | copy-start | bytes 25165828
  0.0 2.3 %copy-start.2 = (f32[2,256,2048]{2,1,0:T(8,128)S(1)}, f32[2,256,2048]{2,1,0:T(8,128)}, u32[]{:S(2)}) copy-start(f32[2,256,2048]{2,1,0:T(8,128)} %x_ref.1) | copy-start | bytes 12582916
  2.3 1.5 %copy-start.3 = (bf16[2048,256]{1,0:T(8,128)(2,1)S(1)}, bf16[2048,256]{1,0:T(8,128)(2,1)}, u32[]{:S(2)}) copy-start(bf16[2048,256]{1,0:T(8,128)(2,1)} %constant.7.clone.low_ref) | copy-start | bytes 3145732
  3.8 1.4 %copy-start.4 = (bf16[2048,256]{1,0:T(8,128)(2,1)S(1)}, bf16[2048,256]{1,0:T(8,128)(2,1)}, u32[]{:S(2)}) copy-start(bf16[2048,256]{1,0:T(8,128)(2,1)} %constant.6.clone.high_ref) | copy-start | bytes 3145732
  5.2 0.9 %copy-start.6 = (bf16[512,256]{1,0:T(8,128)(2,1)S(1)}, bf16[512,256]{1,0:T(8,128)(2,1)}, u32[]{:S(2)}) copy-start(bf16[512,256]{1,0:T(8,128)(2,1)} %constant.8.clone.pick_ref) | copy-start | bytes 786436
  40.2 2.3 %copy-start = (f32[4,256,1024]{2,1,0:T(8,128)S(1)}, f32[4,256,1024]{2,1,0:T(8,128)}, u32[]{:S(2)}) copy-start(f32[4,256,1024]{2,1,0:T(8,128)} %w_ref.7) | copy-start | bytes 12582916
  42.4 1.3 %collective-permute-start = (f32[64,256]{1,0:T(8,128)S(1)}, f32[64,256]{1,0:T(8,128)S(1)}, u32[]{:S(2)}, u32[]{:S(2)}) collective-permute-start(f32[64,256]{1,0:T(8,128)S(1)} %gram.1.c_ref), channel_id=1, source_target_pairs={{0,1},{1,0},{2,3},{3,2},{4,5},{5,4},{6,7},{7,6},{8,9},{9,8},{10,11... | collective-permute-start | bytes 196616 | tf_op jit(solution)/shard_map/ppermute | solution.py:264
  44.0 4.3 %collective-permute-start.1 = (f32[64,256]{1,0:T(8,128)S(1)}, f32[64,256]{1,0:T(8,128)S(1)}, u32[]{:S(2)}, u32[]{:S(2)}) collective-permute-start(f32[64,256]{1,0:T(8,128)S(1)} %join_part.3.c_ref), channel_id=1, source_target_pairs={{0,2},{1,3},{2,0},{3,1},{4,6},{5,7},{6,4},{7,5},{8,10},{9,11},{10,... | collective-permute-start | bytes 196616 | tf_op jit(solution)/shard_map/ppermute | solution.py:264
  48.6 10.5 %copy-start.5 = (f32[256,512]{1,0:T(8,128)S(1)}, f32[256,512]{1,0:T(8,128)}, u32[]{:S(2)}) copy-start(f32[256,512]{1,0:T(8,128)} %e_ref.1) | copy-start | bytes 1572868
  48.6 5.8 %collective-permute-start.2 = (f32[64,256]{1,0:T(8,128)S(1)}, f32[64,256]{1,0:T(8,128)S(1)}, u32[]{:S(2)}, u32[]{:S(2)}) collective-permute-start(f32[64,256]{1,0:T(8,128)S(1)} %join_part.4.c_ref), channel_id=1, source_target_pairs={{0,4},{1,5},{2,6},{3,7},{4,0},{5,1},{6,2},{7,3},{8,12},{9,13},{10,... | collective-permute-start | bytes 196616 | tf_op jit(solution)/shard_map/ppermute | solution.py:264
  54.8 4.3 %collective-permute-start.3 = (f32[64,256]{1,0:T(8,128)S(1)}, f32[64,256]{1,0:T(8,128)S(1)}, u32[]{:S(2)}, u32[]{:S(2)}) collective-permute-start(f32[64,256]{1,0:T(8,128)S(1)} %join_part.5.c_ref), channel_id=1, source_target_pairs={{0,8},{1,9},{2,10},{3,11},{4,12},{5,13},{6,14},{7,15},{8,0},{9,1},... | collective-permute-start | bytes 196616 | tf_op jit(solution)/shard_map/ppermute | solution.py:264
where the time goes:
time: 71 us; the launch traced here: 70.9 us
  blocking collectives  40.5 us (57%)
  waiting for transfers between devices  13.3 us (19%)
  Pallas kernels  9.62 us (14%)
  local copies, waits for them, and re-layouts  6.15 us (9%)
  starting transfers between devices  1.22 us (2%)
    all_to_all x1, blocking collectives, body(): lax.all_to_all(blocks, ('freq', 'trace'), split_axis=0, concat_axis=0, ti...  30.3 us
    ppermute x4, waiting for transfers between devices, from_partner(): lax.ppermute(block, axis, [(at, at ^ 1 << apart) for at in range(count)])  13.3 us
    all_to_all x1, blocking collectives, body(): out = lax.all_to_all(out, 'freq', split_axis=0, concat_axis=0, tiled=True)  10.1 us
    unnamed x14, local copies, waits for them, and re-layouts  6.15 us
    pallas_call x1, Pallas kernels, trace_blocks(): pl.pallas_call(functools.partial(trace_kernel, keep, tone), grid=(steps,)...  3.71 us
    pallas_call x1, Pallas kernels, gram(): pl.pallas_call(gram_kernel, grid=(steps,), in_specs=[pl.BlockSpec((sender...  2.17 us
  transfers between devices with their start and end apart: 4, of which 4 were waited for; matrix products, arithmetic and copies ran while one was open for 0% of the time, Pallas kernels for 2%

commit v1 on v0

--- a/solution.py
+++ b/solution.py
@@ -68,61 +68,106 @@
     return result
 
 
-def trace_kernel(keep, tone, x_ref, high_ref, low_ref, pick_ref, out_ref):
-    rows = x_ref.shape[1]
-    x = jnp.concatenate([x_ref[0], x_ref[1]], axis=0)
-    total = x[:, :128]
-    for at in range(128, x.shape[1], 128):
-        total = total + x[:, at : at + 128]
+def trace_kernel(keep, tone, freq_count, x_hbm, high_hbm, low_hbm, pick_hbm, out_ref, *scratch):
+    x_ref, high_ref, low_ref, pick_ref, imag_ref, real_ref, total_ref, x_sem, table_sem = scratch
+    shots, offsets, samples = x_hbm.shape
+    rows = shots * offsets
+    wide = x_ref.shape[2]
+    count = samples // wide
+    heads = pick_hbm.shape[0] // wide
+    copies = []
+    for at in range(count):
+        part = pl.ds(at * wide, wide)
+        group = [
+            pltpu.make_async_copy(x_hbm.at[s, :, part], x_ref.at[at, pl.ds(s * offsets, offsets)], x_sem.at[at, s])
+            for s in range(shots)
+        ]
+        group.append(pltpu.make_async_copy(high_hbm.at[part], high_ref.at[part], table_sem.at[at, 0]))
+        group.append(pltpu.make_async_copy(low_hbm.at[part], low_ref.at[part], table_sem.at[at, 1]))
+        if at < heads:
+            group.append(
+                pltpu.make_async_copy(pick_hbm.at[part], pick_ref.at[part], table_sem.at[at, 2])
+            )
+        copies.append(group)
+        for copy in group:
+            copy.start()
+    for at in range(count):
+        part = slice(at * wide, at * wide + wide)
+        for copy in copies[at]:
+            copy.wait()
+        x = x_ref[at]
+        total = x[:, :128]
+        for lane in range(128, wide, 128):
+            total = total + x[:, lane : lane + 128]
+        pair = split(x)
+        imag = mm3(pair, (high_ref[part], low_ref[part]), NN)
+        if at < heads:
+            both = mm(jnp.concatenate(pair, axis=0), pick_ref[part], NN)
+            real = (both[:rows] + both[rows:]) * keep
+        if at == 0:
+            imag_ref[...] = imag
+            real_ref[...] = real
+            total_ref[...] = total
+        else:
+            imag_ref[...] += imag
+            total_ref[...] += total
+            if at < heads:
+                real_ref[...] += real
+    total = total_ref[...]
     odd = lax.broadcasted_iota(jnp.int32, total.shape, 1) % 2 == 1
-    mean = jnp.sum(jnp.where(odd, total, 0.0), axis=1, keepdims=True) * tone
-    pair = split(x)
-    imag = mm3(pair, (high_ref[...], low_ref[...]), NN)
-    head = pick_ref.shape[0]
-    both = mm(jnp.concatenate([p[:, :head] for p in pair], axis=0), pick_ref[...], NN)
-    real = (both[: 2 * rows] + both[2 * rows :]) * keep + mean
+    real_ref[...] += jnp.sum(jnp.where(odd, total, 0.0), axis=1, keepdims=True) * tone
+    core = lax.axis_index("trace") % 2
+    pairs, _, box, lanes = out_ref.shape
+    boxes = offsets // box
     for tile in range(TAUS // 128):
-        lanes = slice(128 * tile, 128 * tile + 128)
-        parts = [real[:rows, lanes], imag[:rows, lanes], real[rows:, lanes], imag[rows:, lanes]]
+        cols = slice(128 * tile, 128 * tile + 128)
+        parts = []
+        for s in range(shots):
+            own = slice(s * offsets, s * offsets + offsets)
+            parts += [real_ref[own, cols], imag_ref[own, cols]]
         for q, block in enumerate(move_groups(parts, 32)):
-            out_ref[4 * tile + q] = block.reshape(out_ref.shape[1:])
+            block = block.reshape(boxes // 2, 2, box, lanes)
+            first = (4 * tile + q) * (boxes // 2)
+            for side in range(2):
+                out_ref[pl.ds(first, boxes // 2), side ^ core] = block[:, side]
 
 
 def trace_blocks(traces, freq_count, trace_count):
     shots, offsets, samples = traces.shape
     box = offsets // trace_count
-    steps = 4
+    wide = 256
+    rows = shots * offsets
     high, low, pick, keep, tone = tables(samples, freq_count)
-    whole = lambda a: pl.BlockSpec(a.shape, lambda i: (0, 0))
-    return pl.pallas_call(
-        functools.partial(trace_kernel, keep, tone),
-        grid=(steps,),
-        in_specs=[
-            pl.BlockSpec((shots, offsets // steps, samples), lambda i: (0, i, 0)),
-            whole(high),
-            whole(low),
-            whole(pick),
+    return pl.pallas_call(
+        functools.partial(trace_kernel, keep, tone, freq_count),
+        in_specs=[pl.BlockSpec(memory_space=pltpu.HBM)] * 4,
+        out_specs=pl.BlockSpec(memory_space=pltpu.VMEM),
+        out_shape=jax.ShapeDtypeStruct((freq_count * trace_count // 2, 2, box, 128), F32),
+        scratch_shapes=[
+            pltpu.VMEM((samples // wide, rows, wide), F32),
+            pltpu.VMEM(high.shape, BF16),
+            pltpu.VMEM(low.shape, BF16),
+            pltpu.VMEM(pick.shape, BF16),
+            pltpu.VMEM((rows, TAUS), F32),
+            pltpu.VMEM((rows, TAUS), F32),
+            pltpu.VMEM((rows, 128), F32),
+            pltpu.SemaphoreType.DMA((samples // wide, shots)),
+            pltpu.SemaphoreType.DMA((samples // wide, 3)),
         ],
-        out_specs=pl.BlockSpec(
-            (freq_count, trace_count // steps, box, 128), lambda i: (0, i, 0, 0)
-        ),
-        out_shape=jax.ShapeDtypeStruct((freq_count, trace_count, box, 128), F32),
-        compiler_params=pltpu.CompilerParams(vmem_limit_bytes=32 << 20),
+        compiler_params=pltpu.CompilerParams(vmem_limit_bytes=58 << 20),
         name="trace_blocks",
     )(traces, jnp.asarray(high), jnp.asarray(low), jnp.asarray(pick))
 
 
-def gram_kernel(values_ref, source_ref, out_ref, acc_ref):
+def gram_kernel(values_ref, source_ref, before_ref, out_ref, acc_ref):
     step = pl.program_id(0)
-    depth = values_ref.shape[0] * values_ref.shape[1]
-    turned = values_ref[...].reshape(depth, 128).T
-    pair = split(turned)
+    depth = values_ref.shape[0] * values_ref.shape[2]
+    pair = split(values_ref[...].reshape(depth, 128).T)
     source = source_ref[...]
-    source = source.reshape(source.shape[0] // 2, 2, *source.shape[1:])
     acc = None
     for shot in range(2):
         rows = slice(64 * shot, 64 * shot + 64)
-        weights = split(source[:, shot].reshape(depth, source.shape[3]))
+        weights = split(source[:, 0, shot].reshape(depth, source.shape[4]))
         term = mm3((pair[0][rows], pair[1][rows]), weights, NN)
         acc = term if acc is None else acc + term
 
@@ -136,7 +181,39 @@
 
     @pl.when(step == pl.num_programs(0) - 1)
     def _():
-        out_ref[...] = turn(acc_ref[...])
+        both = turn(acc_ref[...])
+        out_ref[...] = both if before_ref is None else both + before_ref[...]
+
+
+def gram(values, sources, core, before):
+    senders, _, box, lanes = values.shape
+    width = sources.shape[4]
+    steps = 4
+    start = before is None
+    kernel = gram_kernel
+    in_specs = [
+        pl.BlockSpec((senders // steps, 1, box, lanes), lambda i, c: (i, 0, 0, 0)),
+        pl.BlockSpec((senders // steps, 1, 2, box, width), lambda i, c: (i, c[0], 0, 0, 0)),
+    ]
+    if start:
+        kernel = lambda c, v, s, o, a: gram_kernel(v, s, None, o, a)
+    else:
+        kernel = lambda c, v, s, b, o, a: gram_kernel(v, s, b, o, a)
+        in_specs.append(pl.BlockSpec((64, width // 2), lambda i, c: (0, 0)))
+    return pl.pallas_call(
+        kernel,
+        grid_spec=pltpu.PrefetchScalarGridSpec(
+            num_scalar_prefetch=1,
+            grid=(steps,),
+            in_specs=in_specs,
+            out_specs=pl.BlockSpec((64, width // 2), lambda i, c: (0, 0)),
+            scratch_shapes=[pltpu.VMEM((64, width), F32)],
+        ),
+        out_shape=jax.ShapeDtypeStruct((64, width // 2), F32),
+        compiler_params=pltpu.CompilerParams(vmem_limit_bytes=53 << 20),
+        cost_estimate=pl.CostEstimate(flops=2 * 10**9, bytes_accessed=10**7, transcendentals=0),
+        name="gram_first" if start else "gram_second",
+    )(core, values, sources, *(() if start else (before,)))
 
 
 def turn(both):
@@ -144,25 +221,6 @@
     real = both[:half, :width] - both[half:, width:]
     imag = both[half:, :width] + both[:half, width:]
     return jnp.concatenate([real, imag], axis=0)
-
-
-def gram(values, sources):
-    senders, box, lanes = values.shape
-    shots, _, width = sources.shape
-    steps = 4
-    return pl.pallas_call(
-        gram_kernel,
-        grid=(steps,),
-        in_specs=[
-            pl.BlockSpec((senders // steps, box, lanes), lambda i: (i, 0, 0)),
-            pl.BlockSpec((shots // steps, box, width), lambda i: (i, 0, 0)),
-        ],
-        out_specs=pl.BlockSpec((64, width // 2), lambda i: (0, 0)),
-        out_shape=jax.ShapeDtypeStruct((64, width // 2), F32),
-        scratch_shapes=[pltpu.VMEM((64, width), F32)],
-        compiler_params=pltpu.CompilerParams(vmem_limit_bytes=32 << 20),
-        name="gram",
-    )(values, sources)
 
 
 def own_kernel(c_ref, w_ref, own_ref, high_ref, low_ref):
@@ -268,9 +326,16 @@
     freq_count = lax.axis_size("freq")
     trace_count = lax.axis_size("trace")
     blocks = trace_blocks(traces, freq_count, trace_count)
-    blocks = blocks.reshape(freq_count * trace_count, *blocks.shape[2:])
-    values = lax.all_to_all(blocks, ("freq", "trace"), split_axis=0, concat_axis=0, tiled=True)
-    c = gram(values, source_weights)
+    every = range(freq_count * trace_count)
+    groups = [[d for d in every if d % 2 == side] for side in range(2)]
+    blocks = lax.all_to_all(
+        blocks, ("freq", "trace"), 0, 0, axis_index_groups=groups, tiled=True
+    )
+    crossed = from_partner(blocks[:, 1:], "trace", 0)
+    core = (lax.axis_index("trace") % 2).reshape(1)
+    sources = source_weights.reshape(blocks.shape[0], 2, 2, *source_weights.shape[1:])
+    c = gram(blocks[:, :1], sources, core, None)
+    c = gram(crossed, sources, 1 - core, c)
     levels = level_weights.shape[0]
     for level in range(levels):
         partner = from_partner(c, "trace", level)

time: 71 us -> 74.2 us (1.045)
  Pallas kernels: 9.62 us -> 18.4 us
  local copies, waits for them, and re-layouts: 6.15 us -> 0.09 us
  starting transfers between devices: 1.22 us -> 3.32 us
  waiting for transfers between devices: 13.3 us -> 11.5 us
    pallas_call x2 -> x3, Pallas kernels: 5.88 us -> 14.7 us  [the longest x2 7.65 us: gram(): pl.pallas_call(kernel, grid_spec=pltpu.PrefetchScalarGridSpec(num_scalar_...]
    unnamed x14 -> x4, local copies, waits for them, and re-layouts: 6.15 us -> 0.01 us
    ppermute x4 -> x5, starting transfers between devices: 1.22 us -> 3.32 us  [from_partner(): lax.ppermute(block, axis, [(at, at ^ 1 << apart) for at in range(count)])]
    ppermute x4 -> x5, waiting for transfers between devices: 13.3 us -> 11.5 us  [from_partner(): lax.ppermute(block, axis, [(at, at ^ 1 << apart) for at in range(count)])]
  transfers between devices with their start and end apart: 4 -> 5, of which waited for: 4 -> 4; matrix products, arithmetic and copies ran while one was open for 0% -> 0% of each run, Pallas kernels for 2% -> 7%
where the time goes in v1:
time: 74.2 us; the launch traced here: 73.9 us
  blocking collectives  40.5 us (55%)
  Pallas kernels  18.4 us (25%)
  waiting for transfers between devices  11.5 us (15%)
  starting transfers between devices  3.32 us (4%)
    all_to_all x1, blocking collectives, body(): lax.all_to_all(blocks, ('freq', 'trace'), 0, 0, axis_index_groups=groups,...  30.1 us
    ppermute x5, waiting for transfers between devices, from_partner(): lax.ppermute(block, axis, [(at, at ^ 1 << apart) for at in range(count)])  11.5 us
    all_to_all x1, blocking collectives, body(): out = lax.all_to_all(out, 'freq', split_axis=0, concat_axis=0, tiled=True)  10.4 us
    pallas_call x2, Pallas kernels, gram(): pl.pallas_call(kernel, grid_spec=pltpu.PrefetchScalarGridSpec(num_scalar_...  7.65 us
    pallas_call x1, Pallas kernels, trace_blocks(): pl.pallas_call(functools.partial(trace_kernel, keep, tone, freq_count), i...  7.01 us
    ppermute x5, starting transfers between devices, from_partner(): lax.ppermute(block, axis, [(at, at ^ 1 << apart) for at in range(count)])  3.32 us
  transfers between devices with their start and end apart: 5, of which 4 were waited for; matrix products, arithmetic and copies ran while one was open for 0% of the time, Pallas kernels for 7%

profile of v1, /device:TPU:0, one launch (start us, length us, event | category | flops | bytes accessed | tf_op | source)
XLA Modules:
  0.0 73.9 jit_solution(7906226463547101262)
XLA Ops:
  0.0 7.0 %trace_blocks.1 = f32[64,2,16,128]{3,2,1,0:T(8,128)} custom-call(f32[2,256,2048]{2,1,0:T(8,128)} %x_hbm.1, bf16[2048,256]{1,0:T(8,128)(2,1)} %constant.25.clone.high_hbm, bf16[2048,256]{1,0:T(8,128)(2,1)} %constant.26.clone.low_hbm, bf16[512,256]{1,0:T(8,128)(2,1)} %constant.27.clone.pick_hbm), custom_call_target="tpu_custom_call" | custom-call | tf_op jit(solution)/shard_map/trace_blocks/pallas_call | solution.py:141
  7.0 30.1 %all_to_all.10 = f32[64,2,16,128]{3,2,1,0:T(8,128)S(1)} all-to-all(f32[64,2,16,128]{3,2,1,0:T(8,128)} %trace_blocks.1), channel_id=1, replica_groups={{0,2,4,6,8,10,12,14,16,18,20,22,24,26,28,30,32,34,36,38,40,42,44,46,48,..., dimensions={0} | all-to-all | bytes 2097152 | tf_op jit(solution)/shard_map/all_to_all | solution.py:331
  37.1 0.1 fusion
  37.2 0.1 collective-permute-start
  37.3 3.7 %gram_first.1.b = f32[64,256]{1,0:T(8,128)S(1)} custom-call(s32[1]{0:T(128)} %bitcast.c, f32[64,1,16,128]{3,2,1,0:T(8,128)S(1)} %get-tuple-element.29.v, f32[64,2,2,16,512]{4,3,2,1,0:T(8,128)} %bitcast.2), custom_call_target="tpu_custom_call" | custom-call | flops 2000000000 | bytes 10000000 | tf_op jit(solution)/shard_map/gram_first/pallas_call | solution.py:203
  41.0 0.0 copy-start
  41.0 0.0 collective-permute-done.v
  41.0 3.9 %gram_second.1.c_ref = f32[64,256]{1,0:T(8,128)S(1)} custom-call(s32[1]{0:T(128)S(6)} %sub.3.c, f32[64,1,16,128]{3,2,1,0:T(8,128)S(1)} %collective-permute-done.v, f32[64,2,2,16,512]{4,3,2,1,0:T(8,128)} %bitcast.3, f32[64,256]{1,0:T(8,128)S(1)} %gram_first.1.b), custom_call_target="tpu_custom_call" | custom-call | flops 2000000000 | bytes 10000000 | tf_op jit(solution)/shard_map/gram_second/pallas_call | solution.py:203
  45.0 0.6 collective-permute-start.1
  45.5 0.0 copy-done
  45.5 0.3 own_part.4
  45.9 0.6 collective-permute-done.1.c_ref
  46.4 0.3 join_part.3.c_ref
  46.7 0.7 collective-permute-start.2
  47.4 0.3 own_part.5
  47.7 3.4 %collective-permute-done.2.c_ref = f32[64,256]{1,0:T(8,128)S(1)} collective-permute-done((f32[64,256]{1,0:T(8,128)S(1)}, f32[64,256]{1,0:T(8,128)S(1)}, u32[]{:S(2)}, u32[]{:S(2)}) %collective-permute-start.2) | collective-permute-done | bytes 65568 | tf_op jit(solution)/shard_map/ppermute | solution.py:322
  51.1 0.3 join_part.4.c_ref
  51.4 0.0 copy-start.1
  51.4 1.5 %collective-permute-start.3 = (f32[64,256]{1,0:T(8,128)S(1)}, f32[64,256]{1,0:T(8,128)S(1)}, u32[]{:S(2)}, u32[]{:S(2)}) collective-permute-start(f32[64,256]{1,0:T(8,128)S(1)} %join_part.4.c_ref), channel_id=1, source_target_pairs={{0,4},{1,5},{2,6},{3,7},{4,0},{5,1},{6,2},{7,3},{8,12},{9,13},{10,... | collective-permute-start | bytes 196616 | tf_op jit(solution)/shard_map/ppermute | solution.py:322
  53.0 0.3 own_part.6
  53.3 4.0 %collective-permute-done.3.c_ref = f32[64,256]{1,0:T(8,128)S(1)} collective-permute-done((f32[64,256]{1,0:T(8,128)S(1)}, f32[64,256]{1,0:T(8,128)S(1)}, u32[]{:S(2)}, u32[]{:S(2)}) %collective-permute-start.3) | collective-permute-done | bytes 65568 | tf_op jit(solution)/shard_map/ppermute | solution.py:322
  57.3 0.3 join_part.5.c_ref
  57.6 0.5 collective-permute-start.4
  58.1 0.3 own_part.7
  58.4 3.5 %collective-permute-done.4.c_ref = f32[64,256]{1,0:T(8,128)S(1)} collective-permute-done((f32[64,256]{1,0:T(8,128)S(1)}, f32[64,256]{1,0:T(8,128)S(1)}, u32[]{:S(2)}, u32[]{:S(2)}) %collective-permute-start.4) | collective-permute-done | bytes 65568 | tf_op jit(solution)/shard_map/ppermute | solution.py:322
  61.9 0.0 copy-done.1
  61.9 0.8 %last_part.1 = f32[8,8,128]{2,1,0:T(8,128)S(1)} custom-call(f32[64,256]{1,0:T(8,128)S(1)} %get-tuple-element.26.own_ref, f32[64,256]{1,0:T(8,128)S(1)} %collective-permute-done.4.c_ref, bf16[512,256]{1,0:T(8,128)(2,1)S(1)} %get-tuple-element.27.high_ref, bf16[512,256]{1,0:T(8,128)(2,1)S(1)} %get-tuple-element.28.low_ref, f32[256,512]{1,0:T(8,128)S(1)} %copy-done.1), custom_call_target="tpu_custom_call" | custom-call | tf_op jit(solution)/shard_map/last_part/pallas_call | solution.py:291
  62.7 10.4 %all_to_all.11.x_ref = f32[8,8,128]{2,1,0:T(8,128)S(1)} all-to-all(f32[8,8,128]{2,1,0:T(8,128)S(1)} %last_part.1), channel_id=1, replica_groups=mesh['freq'=8,'trace'=16] {'freq'}, dimensions={0} | all-to-all | bytes 65536 | tf_op jit(solution)/shard_map/all_to_all | solution.py:347
  73.1 0.8 %final_part.1 = f32[32,256]{1,0:T(8,128)} custom-call(f32[8,8,128]{2,1,0:T(8,128)S(1)} %all_to_all.11.x_ref), custom_call_target="tpu_custom_call" | custom-call | tf_op jit(solution)/shard_map/final_part/pallas_call | solution.py:312
Async XLA Ops:
  37.2 3.9 %collective-permute-start = (f32[64,1,16,128]{3,2,1,0:T(8,128)S(1)}, f32[64,1,16,128]{3,2,1,0:T(8,128)S(1)}, u32[]{:S(2)}, u32[]{:S(2)}) collective-permute-start(f32[64,1,16,128]{3,2,1,0:T(8,128)S(1)} %get-tuple-element.30), channel_id=1, source_target_pairs={{0,1},{1,0},{2,3},{3,2},{4,5},{5,4},{6,7},{7,6},{8,9},{9,8},{10,11... | collective-permute-start | bytes 1572872 | tf_op jit(solution)/shard_map/ppermute | solution.py:322
  41.0 4.5 %copy-start = (f32[4,256,1024]{2,1,0:T(8,128)S(1)}, f32[4,256,1024]{2,1,0:T(8,128)}, u32[]{:S(2)}) copy-start(f32[4,256,1024]{2,1,0:T(8,128)} %w_ref.7) | copy-start | bytes 12582916
  45.0 1.5 %collective-permute-start.1 = (f32[64,256]{1,0:T(8,128)S(1)}, f32[64,256]{1,0:T(8,128)S(1)}, u32[]{:S(2)}, u32[]{:S(2)}) collective-permute-start(f32[64,256]{1,0:T(8,128)S(1)} %gram_second.1.c_ref), channel_id=1, source_target_pairs={{0,1},{1,0},{2,3},{3,2},{4,5},{5,4},{6,7},{7,6},{8,9},{9,8},{10,11... | collective-permute-start | bytes 196616 | tf_op jit(solution)/shard_map/ppermute | solution.py:322
  46.7 4.4 %collective-permute-start.2 = (f32[64,256]{1,0:T(8,128)S(1)}, f32[64,256]{1,0:T(8,128)S(1)}, u32[]{:S(2)}, u32[]{:S(2)}) collective-permute-start(f32[64,256]{1,0:T(8,128)S(1)} %join_part.3.c_ref), channel_id=1, source_target_pairs={{0,2},{1,3},{2,0},{3,1},{4,6},{5,7},{6,4},{7,5},{8,10},{9,11},{10,... | collective-permute-start | bytes 196616 | tf_op jit(solution)/shard_map/ppermute | solution.py:322
  51.4 10.5 %copy-start.1 = (f32[256,512]{1,0:T(8,128)S(1)}, f32[256,512]{1,0:T(8,128)}, u32[]{:S(2)}) copy-start(f32[256,512]{1,0:T(8,128)} %e_ref.1) | copy-start | bytes 1572868
  51.4 5.8 %collective-permute-start.3 = (f32[64,256]{1,0:T(8,128)S(1)}, f32[64,256]{1,0:T(8,128)S(1)}, u32[]{:S(2)}, u32[]{:S(2)}) collective-permute-start(f32[64,256]{1,0:T(8,128)S(1)} %join_part.4.c_ref), channel_id=1, source_target_pairs={{0,4},{1,5},{2,6},{3,7},{4,0},{5,1},{6,2},{7,3},{8,12},{9,13},{10,... | collective-permute-start | bytes 196616 | tf_op jit(solution)/shard_map/ppermute | solution.py:322
  57.6 4.3 %collective-permute-start.4 = (f32[64,256]{1,0:T(8,128)S(1)}, f32[64,256]{1,0:T(8,128)S(1)}, u32[]{:S(2)}, u32[]{:S(2)}) collective-permute-start(f32[64,256]{1,0:T(8,128)S(1)} %join_part.5.c_ref), channel_id=1, source_target_pairs={{0,8},{1,9},{2,10},{3,11},{4,12},{5,13},{6,14},{7,15},{8,0},{9,1},... | collective-permute-start | bytes 196616 | tf_op jit(solution)/shard_map/ppermute | solution.py:322

commit v2 on v0

--- a/solution.py
+++ b/solution.py
@@ -32,26 +32,16 @@
     return both[:rows] + both[rows:] + mm(a_pair[0], b_pair[1], dims)
 
 
-def tau_order(freq_count):
-    per = TAUS // freq_count
-    columns = np.arange(TAUS)
-    owner, inner = columns // per, columns % per
-    return (inner // 8) * (8 * freq_count) + owner * 8 + inner % 8
-
-
-def tables(samples, freq_count):
-    taus = tau_order(freq_count)
+def lane_tau(lane):
+    return 64 * (lane % 16 // 8) + 8 * (lane // 16) + lane % 8
+
+
+def cot_table(samples, wide, scale):
     step = samples // (4 * TAUS)
-    scale = 1.0 / math.sqrt(samples) / math.sqrt(FREQS)
-    n = np.arange(samples)[:, None]
-    gap = (step * taus[None, :] - n) % samples
-    odd = gap % 2 == 1
-    cot = np.where(odd, 1.0 / np.tan(np.pi * np.where(odd, gap, 1) / samples), 0.0) * scale
-    cot = cot.astype(np.float32)
-    high = cot.astype(jnp.bfloat16)
-    low = (cot - high.astype(np.float32)).astype(jnp.bfloat16)
-    pick = (gap[: samples // 4] == 0).astype(jnp.bfloat16)
-    return high, low, pick, FREQS * scale, scale
+    taus = lane_tau(np.arange(128))
+    gap = wide * np.arange(samples // wide)[:, None, None] + step * taus
+    gap = gap - (2 * np.arange(wide // 2)[None, :, None] + 1)
+    return (scale / np.tan(np.pi * gap / samples)).astype(np.float32)
 
 
 def move_groups(parts, width):
@@ -68,48 +58,99 @@
     return result
 
 
-def trace_kernel(keep, tone, x_ref, high_ref, low_ref, pick_ref, out_ref):
-    rows = x_ref.shape[1]
-    x = jnp.concatenate([x_ref[0], x_ref[1]], axis=0)
+def trace_kernel(scale, x_hbm, table_hbm, out_ref, x_ref, table_ref, full_ref, x_sem, table_sem):
+    shots, offsets, samples = x_hbm.shape
+    count, wide, _ = full_ref.shape
+    rows = shots * offsets
+    copies = [
+        pltpu.make_async_copy(x_hbm.at[s], x_ref.at[pl.ds(s * offsets, offsets)], x_sem.at[s])
+        for s in range(shots)
+    ]
+    table_copy = pltpu.make_async_copy(table_hbm, table_ref, table_sem)
+    table_copy.start()
+    for copy in copies:
+        copy.start()
+    lane = lax.broadcasted_iota(jnp.int32, (wide, 128), 1)
+    row = lax.broadcasted_iota(jnp.int32, (wide, 128), 0)
+    step = samples // (4 * TAUS)
+    pick = jnp.where(row == step * lane_tau(lane), 1.0, 0.0).astype(BF16)
+    full_ref[...] = jnp.zeros_like(full_ref)
+    table_copy.wait()
+    for d in range(count):
+        full_ref[d, pl.ds(1, wide // 2, 2), :] = table_ref[d]
+    table = [split(full_ref[d]) for d in range(count)]
+    right = [
+        jnp.concatenate(
+            [
+                jnp.concatenate([table[-at % count][part], table[(1 - at) % count][part]], axis=1)
+                for at in range(count)
+            ],
+            axis=0,
+        )
+        for part in range(2)
+    ]
+    for copy in copies:
+        copy.wait()
+    x = x_ref[...]
     total = x[:, :128]
-    for at in range(128, x.shape[1], 128):
+    for at in range(128, samples, 128):
         total = total + x[:, at : at + 128]
+    pair = split(x)
+    imag = mm3(pair, right, NN)
     odd = lax.broadcasted_iota(jnp.int32, total.shape, 1) % 2 == 1
-    mean = jnp.sum(jnp.where(odd, total, 0.0), axis=1, keepdims=True) * tone
-    pair = split(x)
-    imag = mm3(pair, (high_ref[...], low_ref[...]), NN)
-    head = pick_ref.shape[0]
-    both = mm(jnp.concatenate([p[:, :head] for p in pair], axis=0), pick_ref[...], NN)
-    real = (both[: 2 * rows] + both[2 * rows :]) * keep + mean
-    for tile in range(TAUS // 128):
-        lanes = slice(128 * tile, 128 * tile + 128)
-        parts = [real[:rows, lanes], imag[:rows, lanes], real[rows:, lanes], imag[rows:, lanes]]
-        for q, block in enumerate(move_groups(parts, 32)):
-            out_ref[4 * tile + q] = block.reshape(out_ref.shape[1:])
+    mean = jnp.sum(jnp.where(odd, total, 0.0), axis=1, keepdims=True) * scale
+    real = []
+    for half in range(2):
+        part = slice(half * wide, half * wide + wide)
+        both = mm(jnp.concatenate([p[:, part] for p in pair], axis=0), pick, NN)
+        real.append((both[:rows] + both[rows:]) * (FREQS * scale) + mean)
+    parts = []
+    for s in range(shots):
+        own = slice(s * offsets, s * offsets + offsets)
+        parts += [real[0][own], real[1][own], imag[own, :128], imag[own, 128:]]
+    for r, block in enumerate(move_groups(parts, 16)):
+        out_ref[r] = block.reshape(out_ref.shape[1:])
 
 
 def trace_blocks(traces, freq_count, trace_count):
     shots, offsets, samples = traces.shape
-    box = offsets // trace_count
-    steps = 4
-    high, low, pick, keep, tone = tables(samples, freq_count)
-    whole = lambda a: pl.BlockSpec(a.shape, lambda i: (0, 0))
-    return pl.pallas_call(
-        functools.partial(trace_kernel, keep, tone),
-        grid=(steps,),
-        in_specs=[
-            pl.BlockSpec((shots, offsets // steps, samples), lambda i: (0, i, 0)),
-            whole(high),
-            whole(low),
-            whole(pick),
-        ],
-        out_specs=pl.BlockSpec(
-            (freq_count, trace_count // steps, box, 128), lambda i: (0, i, 0, 0)
+    wide = samples // 8
+    scale = 1.0 / math.sqrt(samples) / math.sqrt(FREQS)
+    table = jnp.asarray(cot_table(samples, wide, scale))
+    return pl.pallas_call(
+        functools.partial(trace_kernel, scale),
+        in_specs=[pl.BlockSpec(memory_space=pltpu.HBM)] * 2,
+        out_specs=pl.BlockSpec(memory_space=pltpu.VMEM),
+        out_shape=jax.ShapeDtypeStruct(
+            (freq_count, trace_count, offsets // trace_count, 128), F32
         ),
-        out_shape=jax.ShapeDtypeStruct((freq_count, trace_count, box, 128), F32),
+        scratch_shapes=[
+            pltpu.VMEM((shots * offsets, samples), F32),
+            pltpu.VMEM(table.shape, F32),
+            pltpu.VMEM((samples // wide, wide, 128), F32),
+            pltpu.SemaphoreType.DMA((shots,)),
+            pltpu.SemaphoreType.DMA,
+        ],
         compiler_params=pltpu.CompilerParams(vmem_limit_bytes=32 << 20),
         name="trace_blocks",
-    )(traces, jnp.asarray(high), jnp.asarray(low), jnp.asarray(pick))
+    )(*(pltpu.with_memory_space_constraint(a, pltpu.HBM) for a in (traces, table)))
+
+
+def hold_kernel(x_ref, out_ref):
+    pass
+
+
+def hold(x):
+    return pl.pallas_call(
+        hold_kernel,
+        in_specs=[pl.BlockSpec(memory_space=pl.ANY)],
+        out_specs=pl.BlockSpec(memory_space=pl.ANY),
+        out_shape=jax.ShapeDtypeStruct(x.shape, x.dtype),
+        input_output_aliases={0: 0},
+        compiler_params=pltpu.CompilerParams(vmem_limit_bytes=1 << 20),
+        cost_estimate=pl.CostEstimate(flops=2 * 10**10, bytes_accessed=100 << 20, transcendentals=0),
+        name="hold",
+    )(x)
 
 
 def gram_kernel(values_ref, source_ref, out_ref, acc_ref):
@@ -149,7 +190,7 @@
 def gram(values, sources):
     senders, box, lanes = values.shape
     shots, _, width = sources.shape
-    steps = 4
+    steps = 2
     return pl.pallas_call(
         gram_kernel,
         grid=(steps,),
@@ -269,6 +310,7 @@
     trace_count = lax.axis_size("trace")
     blocks = trace_blocks(traces, freq_count, trace_count)
     blocks = blocks.reshape(freq_count * trace_count, *blocks.shape[2:])
+    blocks = hold(hold(blocks))
     values = lax.all_to_all(blocks, ("freq", "trace"), split_axis=0, concat_axis=0, tiled=True)
     c = gram(values, source_weights)
     levels = level_weights.shape[0]

time: 71 us -> 66 us (0.930)
  local copies, waits for them, and re-layouts: 6.15 us -> 0.13 us
  Pallas kernels: 9.62 us -> 10.6 us
    unnamed x14 -> x8, local copies, waits for them, and re-layouts: 6.15 us -> 0.13 us
    pallas_call x1 -> x3, Pallas kernels: 3.71 us -> 4.94 us  [the longest x1 4.93 us: trace_blocks(): pl.pallas_call(functools.partial(trace_kernel, scale), in_specs=[pl.Block...]
where the time goes in v2:
time: 66 us; the launch traced here: 65.8 us
  blocking collectives  40.5 us (61%)
  waiting for transfers between devices  13.2 us (20%)
  Pallas kernels  10.6 us (16%)
  starting transfers between devices  1.23 us (2%)
    all_to_all x1, blocking collectives, body(): lax.all_to_all(blocks, ('freq', 'trace'), split_axis=0, concat_axis=0, ti...  30.3 us
    ppermute x4, waiting for transfers between devices, from_partner(): lax.ppermute(block, axis, [(at, at ^ 1 << apart) for at in range(count)])  13.2 us
    all_to_all x1, blocking collectives, body(): out = lax.all_to_all(out, 'freq', split_axis=0, concat_axis=0, tiled=True)  10.1 us
    pallas_call x1, Pallas kernels, trace_blocks(): pl.pallas_call(functools.partial(trace_kernel, scale), in_specs=[pl.Block...  4.93 us
    pallas_call x1, Pallas kernels, gram(): pl.pallas_call(gram_kernel, grid=(steps,), in_specs=[pl.BlockSpec((sender...  1.98 us
  transfers between devices with their start and end apart: 4, of which 4 were waited for; matrix products, arithmetic and copies ran while one was open for 0% of the time, Pallas kernels for 2%

profile of v2, /device:TPU:0, one launch (start us, length us, event | category | flops | bytes accessed | tf_op | source)
XLA Modules:
  0.0 65.8 jit_solution(2872851792947247361)
XLA Ops:
  0.0 4.9 %trace_blocks.1 = f32[8,16,16,128]{3,2,1,0:T(8,128)S(1)} custom-call(f32[2,256,2048]{2,1,0:T(8,128)} %x_hbm.1, f32[8,128,128]{2,1,0:T(8,128)} %constant.2.clone.table_hbm), custom_call_target="tpu_custom_call" | custom-call | tf_op jit(solution)/shard_map/trace_blocks/pallas_call | solution.py:120
  4.9 0.0 slice-start
  5.0 0.0 slice-start.1
  5.0 30.3 %all_to_all.10.values_ref = f32[128,16,128]{2,1,0:T(8,128)S(1)} all-to-all(f32[128,16,128]{2,1,0:T(8,128)S(1)} %hold.3), channel_id=1, replica_groups=mesh['freq'=8,'trace'=16] {'freq','trace'}, dimensions={0} | all-to-all | bytes 2097152 | tf_op jit(solution)/shard_map/all_to_all | solution.py:314
  35.3 0.0 slice-done
  35.3 0.0 slice-done.1
  35.3 0.0 copy-start
  35.3 2.0 %gram.1.c_ref = f32[64,256]{1,0:T(8,128)S(1)} custom-call(f32[128,16,128]{2,1,0:T(8,128)S(1)} %all_to_all.10.values_ref, f32[256,16,512]{2,1,0:T(8,128)S(1)} %bitcast.2), custom_call_target="tpu_custom_call" | custom-call | tf_op jit(solution)/shard_map/gram/pallas_call | solution.py:194
  37.3 0.1 collective-permute-start
  37.4 0.1 copy-done
  37.5 0.3 own_part.4
  37.9 0.8 %collective-permute-done.c_ref = f32[64,256]{1,0:T(8,128)S(1)} collective-permute-done((f32[64,256]{1,0:T(8,128)S(1)}, f32[64,256]{1,0:T(8,128)S(1)}, u32[]{:S(2)}, u32[]{:S(2)}) %collective-permute-start) | collective-permute-done | bytes 65568 | tf_op jit(solution)/shard_map/ppermute | solution.py:305
  38.7 0.3 join_part.3.c_ref
  38.9 0.3 collective-permute-start.1
  39.3 0.3 own_part.5
  39.6 3.7 %collective-permute-done.1.c_ref = f32[64,256]{1,0:T(8,128)S(1)} collective-permute-done((f32[64,256]{1,0:T(8,128)S(1)}, f32[64,256]{1,0:T(8,128)S(1)}, u32[]{:S(2)}, u32[]{:S(2)}) %collective-permute-start.1) | collective-permute-done | bytes 65568 | tf_op jit(solution)/shard_map/ppermute | solution.py:305
  43.3 0.3 join_part.4.c_ref
  43.6 0.0 copy-start.1
  43.6 0.2 collective-permute-start.2
  43.8 0.3 own_part.6
  44.1 5.3 %collective-permute-done.2.c_ref = f32[64,256]{1,0:T(8,128)S(1)} collective-permute-done((f32[64,256]{1,0:T(8,128)S(1)}, f32[64,256]{1,0:T(8,128)S(1)}, u32[]{:S(2)}, u32[]{:S(2)}) %collective-permute-start.2) | collective-permute-done | bytes 65568 | tf_op jit(solution)/shard_map/ppermute | solution.py:305
  49.4 0.3 join_part.5.c_ref
  49.7 0.6 collective-permute-start.3
  50.3 0.3 own_part.7
  50.7 3.4 %collective-permute-done.3.c_ref = f32[64,256]{1,0:T(8,128)S(1)} collective-permute-done((f32[64,256]{1,0:T(8,128)S(1)}, f32[64,256]{1,0:T(8,128)S(1)}, u32[]{:S(2)}, u32[]{:S(2)}) %collective-permute-start.3) | collective-permute-done | bytes 65568 | tf_op jit(solution)/shard_map/ppermute | solution.py:305
  54.1 0.0 copy-done.1
  54.1 0.8 %last_part.1 = f32[8,8,128]{2,1,0:T(8,128)S(1)} custom-call(f32[64,256]{1,0:T(8,128)S(1)} %get-tuple-element.26.own_ref, f32[64,256]{1,0:T(8,128)S(1)} %collective-permute-done.3.c_ref, bf16[512,256]{1,0:T(8,128)(2,1)S(1)} %get-tuple-element.27.high_ref, bf16[512,256]{1,0:T(8,128)(2,1)S(1)} %get-tuple-element.28.low_ref, f32[256,512]{1,0:T(8,128)S(1)} %copy-done.1), custom_call_target="tpu_custom_call" | custom-call | tf_op jit(solution)/shard_map/last_part/pallas_call | solution.py:274
  54.9 10.1 %all_to_all.11.x_ref = f32[8,8,128]{2,1,0:T(8,128)S(1)} all-to-all(f32[8,8,128]{2,1,0:T(8,128)S(1)} %last_part.1), channel_id=1, replica_groups=mesh['freq'=8,'trace'=16] {'freq'}, dimensions={0} | all-to-all | bytes 65536 | tf_op jit(solution)/shard_map/all_to_all | solution.py:324
  65.0 0.8 %final_part.1 = f32[32,256]{1,0:T(8,128)} custom-call(f32[8,8,128]{2,1,0:T(8,128)S(1)} %all_to_all.11.x_ref), custom_call_target="tpu_custom_call" | custom-call | tf_op jit(solution)/shard_map/final_part/pallas_call | solution.py:295
  (3 shorter events, 0.0 us)
Async XLA Ops:
  4.9 30.4 %slice-start = ((s8[8388608]{0:T(1024)(128)(4,1)}), s8[4194304]{0:T(1024)(128)(4,1)S(1)}, s32[]{:S(2)}) async-start(s8[8388608]{0:T(1024)(128)(4,1)} %bitcast.1), calls=%async_computation.2 | async-start | bytes 8388608
  5.0 30.4 %slice-start.1 = ((s8[8388608]{0:T(1024)(128)(4,1)}), s8[4194304]{0:T(1024)(128)(4,1)S(1)}, s32[]{:S(2)}) async-start(s8[8388608]{0:T(1024)(128)(4,1)} %bitcast.1), calls=%async_computation.3 | async-start | bytes 8388608
  35.3 2.2 %copy-start = (f32[4,256,1024]{2,1,0:T(8,128)S(1)}, f32[4,256,1024]{2,1,0:T(8,128)}, u32[]{:S(2)}) copy-start(f32[4,256,1024]{2,1,0:T(8,128)} %w_ref.7) | copy-start | bytes 12582916
  37.3 1.3 %collective-permute-start = (f32[64,256]{1,0:T(8,128)S(1)}, f32[64,256]{1,0:T(8,128)S(1)}, u32[]{:S(2)}, u32[]{:S(2)}) collective-permute-start(f32[64,256]{1,0:T(8,128)S(1)} %gram.1.c_ref), channel_id=1, source_target_pairs={{0,1},{1,0},{2,3},{3,2},{4,5},{5,4},{6,7},{7,6},{8,9},{9,8},{10,11... | collective-permute-start | bytes 196616 | tf_op jit(solution)/shard_map/ppermute | solution.py:305
  38.9 4.3 %collective-permute-start.1 = (f32[64,256]{1,0:T(8,128)S(1)}, f32[64,256]{1,0:T(8,128)S(1)}, u32[]{:S(2)}, u32[]{:S(2)}) collective-permute-start(f32[64,256]{1,0:T(8,128)S(1)} %join_part.3.c_ref), channel_id=1, source_target_pairs={{0,2},{1,3},{2,0},{3,1},{4,6},{5,7},{6,4},{7,5},{8,10},{9,11},{10,... | collective-permute-start | bytes 196616 | tf_op jit(solution)/shard_map/ppermute | solution.py:305
  43.6 10.5 %copy-start.1 = (f32[256,512]{1,0:T(8,128)S(1)}, f32[256,512]{1,0:T(8,128)}, u32[]{:S(2)}) copy-start(f32[256,512]{1,0:T(8,128)} %e_ref.1) | copy-start | bytes 1572868
  43.6 5.8 %collective-permute-start.2 = (f32[64,256]{1,0:T(8,128)S(1)}, f32[64,256]{1,0:T(8,128)S(1)}, u32[]{:S(2)}, u32[]{:S(2)}) collective-permute-start(f32[64,256]{1,0:T(8,128)S(1)} %join_part.4.c_ref), channel_id=1, source_target_pairs={{0,4},{1,5},{2,6},{3,7},{4,0},{5,1},{6,2},{7,3},{8,12},{9,13},{10,... | collective-permute-start | bytes 196616 | tf_op jit(solution)/shard_map/ppermute | solution.py:305
  49.7 4.3 %collective-permute-start.3 = (f32[64,256]{1,0:T(8,128)S(1)}, f32[64,256]{1,0:T(8,128)S(1)}, u32[]{:S(2)}, u32[]{:S(2)}) collective-permute-start(f32[64,256]{1,0:T(8,128)S(1)} %join_part.5.c_ref), channel_id=1, source_target_pairs={{0,8},{1,9},{2,10},{3,11},{4,12},{5,13},{6,14},{7,15},{8,0},{9,1},... | collective-permute-start | bytes 196616 | tf_op jit(solution)/shard_map/ppermute | solution.py:305

commit v3 on v2

--- a/solution.py
+++ b/solution.py
@@ -206,6 +206,38 @@
     )(values, sources)
 
 
+def fold(e, w, first):
+    k = w.shape[0]
+    left = split(jnp.concatenate([e[:, :k], e[:, k:]], axis=0))
+    right = [w[:, at : at + k] for at in (first, first + 2 * k)]
+    both = mm3(left, split(jnp.concatenate(right, axis=1)), NN)
+    real = both[:k, :k] - both[k:, k:]
+    imag = both[:k, k:] + both[k:, :k]
+    return jnp.concatenate([real, imag], axis=1)
+
+
+def far_kernel(e_ref, w_ref, after_ref, out_ref):
+    out_ref[...] = fold(e_ref[...], w_ref[0], w_ref.shape[1])
+
+
+def far_part(e, weights, after):
+    levels, k, width = weights.shape
+    return pl.pallas_call(
+        far_kernel,
+        grid=(1,),
+        in_specs=[
+            pl.BlockSpec(e.shape, lambda i: (0, 0)),
+            pl.BlockSpec((1, k, width), lambda i: (levels - 1, 0, 0)),
+            pl.BlockSpec(memory_space=pl.ANY),
+        ],
+        out_specs=pl.BlockSpec(e.shape, lambda i: (0, 0)),
+        out_shape=jax.ShapeDtypeStruct(e.shape, F32),
+        compiler_params=pltpu.CompilerParams(vmem_limit_bytes=16 << 20),
+        cost_estimate=pl.CostEstimate(flops=5 * 10**8, bytes_accessed=10**6, transcendentals=0),
+        name="far_part",
+    )(e, weights, after)
+
+
 def own_kernel(c_ref, w_ref, own_ref, high_ref, low_ref):
     k = c_ref.shape[1]
     weights = w_ref[0]
@@ -216,29 +248,31 @@
     low_ref[...] = low
 
 
-def own_part(c, weights, level):
+def own_fold_kernel(c_ref, w_ref, e_ref, last_ref, own_ref, high_ref, low_ref, *fold_refs):
+    own_kernel(c_ref, w_ref, own_ref, high_ref, low_ref)
+    for ref, part in zip(fold_refs, split(fold(e_ref[...], last_ref[0], 0))):
+        ref[...] = part
+
+
+def own_part(c, weights, level, e=None):
     rows, k = c.shape
-    return pl.pallas_call(
-        own_kernel,
+    last = weights.shape[0] - 1
+    whole = lambda *shape: pl.BlockSpec(shape, lambda i: (0,) * len(shape))
+    sheet = lambda at: pl.BlockSpec((1, k, 4 * k), lambda i: (at, 0, 0))
+    extra = () if e is None else (e, weights)
+    pairs = [(2 * k, k)] * 2 + ([] if e is None else [e.shape] * 2)
+    return pl.pallas_call(
+        own_kernel if e is None else own_fold_kernel,
         grid=(1,),
-        in_specs=[
-            pl.BlockSpec((rows, k), lambda i: (0, 0)),
-            pl.BlockSpec((1, k, 4 * k), lambda i: (level, 0, 0)),
-        ],
-        out_specs=[
-            pl.BlockSpec((rows, k), lambda i: (0, 0)),
-            pl.BlockSpec((2 * k, k), lambda i: (0, 0)),
-            pl.BlockSpec((2 * k, k), lambda i: (0, 0)),
-        ],
-        out_shape=[
-            jax.ShapeDtypeStruct((rows, k), F32),
-            jax.ShapeDtypeStruct((2 * k, k), BF16),
-            jax.ShapeDtypeStruct((2 * k, k), BF16),
-        ],
+        in_specs=[whole(rows, k), sheet(level)]
+        + ([] if e is None else [whole(*e.shape), sheet(last)]),
+        out_specs=[whole(rows, k)] + [whole(*p) for p in pairs],
+        out_shape=[jax.ShapeDtypeStruct((rows, k), F32)]
+        + [jax.ShapeDtypeStruct(p, BF16) for p in pairs],
         compiler_params=pltpu.CompilerParams(vmem_limit_bytes=16 << 20),
         cost_estimate=pl.CostEstimate(flops=10**8, bytes_accessed=10**6, transcendentals=0),
-        name="own_part",
-    )(c, weights)
+        name="own_part" if e is None else "own_fold_part",
+    )(c, weights, *extra)
 
 
 def joined(own_ref, c_ref, high_ref, low_ref):
@@ -249,16 +283,19 @@
     out_ref[...] = joined(own_ref, c_ref, high_ref, low_ref)
 
 
-def last_kernel(own_ref, c_ref, high_ref, low_ref, e_ref, out_ref):
+def last_kernel(own_ref, c_ref, high_ref, low_ref, near_high, near_low, far_ref, out_ref):
     c = joined(own_ref, c_ref, high_ref, low_ref)
     half = c.shape[0] // 2
-    row = jnp.concatenate([c[:half], -c[half:]], axis=1)
-    values = mm3(split(row), split(e_ref[...]), NT)
-    for tile in range(values.shape[1] // 128):
-        lanes = slice(128 * tile, 128 * tile + 128)
-        parts = [values[8 * g : 8 * g + 8, lanes] for g in range(4)]
-        for q, block in enumerate(move_groups(parts, 32)):
-            out_ref[4 * tile + q] = block
+    row = split(jnp.concatenate([c[:half], -c[half:]], axis=1))
+    side = lax.axis_index("trace") // 8
+    pairs = [(near_high[...], near_low[...]), split(far_ref[...])]
+    for at, pair in enumerate(pairs):
+        values = mm3(row, pair, NT)
+        for tile in range(values.shape[1] // 128):
+            lanes = slice(128 * tile, 128 * tile + 128)
+            parts = [values[8 * g : 8 * g + 8, lanes] for g in range(4)]
+            for q, block in enumerate(move_groups(parts, 32)):
+                out_ref[2 * (4 * tile + q) + (at ^ side)] = block
 
 
 def join_part(own, c, high, low):
@@ -270,17 +307,19 @@
     )(own, c, high, low)
 
 
-def last_part(own, c, high, low, e, freq_count):
+def last_part(own, c, high, low, near_high, near_low, far, freq_count):
     return pl.pallas_call(
         last_kernel,
-        out_shape=jax.ShapeDtypeStruct((freq_count, 8, 128), F32),
+        out_shape=jax.ShapeDtypeStruct((2 * freq_count, 8, 128), F32),
         compiler_params=pltpu.CompilerParams(vmem_limit_bytes=16 << 20),
         name="last_part",
-    )(own, c, high, low, e)
+    )(own, c, high, low, near_high, near_low, far)
 
 
 def final_kernel(x_ref, out_ref):
-    x = x_ref[...].reshape(-1, 128)
+    x = x_ref[...]
+    x = x.reshape(x.shape[0] // 2, 2, 8, 128)
+    x = (x[:, 0] + x[:, 1]).reshape(-1, 128)
     x = jnp.concatenate([x, jnp.zeros_like(x)], axis=0).T
     low = lax.broadcasted_iota(jnp.int32, (32, 128), 1) < 64
     for tile in range(2):
@@ -312,16 +351,26 @@
     blocks = blocks.reshape(freq_count * trace_count, *blocks.shape[2:])
     blocks = hold(hold(blocks))
     values = lax.all_to_all(blocks, ("freq", "trace"), split_axis=0, concat_axis=0, tiled=True)
+    last = level_weights.shape[0] - 1
+    far = from_partner(far_part(slowness_weights, level_weights, values), "trace", last)
     c = gram(values, source_weights)
-    levels = level_weights.shape[0]
-    for level in range(levels):
+    for level in range(last):
         partner = from_partner(c, "trace", level)
-        own, high, low = own_part(c, level_weights, level)
-        if level < levels - 1:
+        if level == 1:
+            own, high, low, *near = own_part(c, level_weights, level, slowness_weights)
+        else:
+            own, high, low = own_part(c, level_weights, level)
+        if level < last - 1:
             c = join_part(own, partner, high, low)
-        else:
-            out = last_part(own, partner, high, low, slowness_weights, freq_count)
-    out = lax.all_to_all(out, "freq", split_axis=0, concat_axis=0, tiled=True)
+    out = last_part(own, partner, high, low, *near, far, freq_count)
+    half = trace_count // 2
+    groups = [
+        [r * trace_count + t * half + rest for r in range(freq_count) for t in range(2)]
+        for rest in range(half)
+    ]
+    out = lax.all_to_all(
+        out, ("freq", "trace"), 0, 0, axis_index_groups=groups, tiled=True
+    )
     return final_part(out)
 
 

time: 66 us -> 63.3 us (0.959)
  waiting for transfers between devices: 13.2 us -> 9.21 us
  blocking collectives: 40.5 us -> 41.2 us
    ppermute x4, waiting for transfers between devices: 13.2 us -> 9.21 us  [from_partner(): lax.ppermute(block, axis, [(at, at ^ 1 << apart) for at in range(count)])]
    pallas_call x5, Pallas kernels: 2.11 us -> 2.88 us  [the longest x3 1.5 us: own_part(): pl.pallas_call(own_kernel if e is None else own_fold_kernel, grid=(1,), i...]
    all_to_all x1, blocking collectives: 10.1 us -> 10.9 us  [body(): lax.all_to_all(out, ('freq', 'trace'), 0, 0, axis_index_groups=groups, ti...]
  transfers between devices with their start and end apart: 4 -> 4, of which waited for: 4 -> 3; matrix products, arithmetic and copies ran while one was open for 0% -> 0% of each run, Pallas kernels for 2% -> 6%
where the time goes in v3:
time: 63.3 us; the launch traced here: 63.1 us
  blocking collectives  41.2 us (65%)
  Pallas kernels  11.1 us (18%)
  waiting for transfers between devices  9.21 us (15%)
  starting transfers between devices  1.4 us (2%)
    all_to_all x1, blocking collectives, body(): lax.all_to_all(blocks, ('freq', 'trace'), split_axis=0, concat_axis=0, ti...  30.3 us
    all_to_all x1, blocking collectives, body(): lax.all_to_all(out, ('freq', 'trace'), 0, 0, axis_index_groups=groups, ti...  10.9 us
    ppermute x4, waiting for transfers between devices, from_partner(): lax.ppermute(block, axis, [(at, at ^ 1 << apart) for at in range(count)])  9.21 us
    pallas_call x1, Pallas kernels, trace_blocks(): pl.pallas_call(functools.partial(trace_kernel, scale), in_specs=[pl.Block...  4.93 us
    pallas_call x1, Pallas kernels, gram(): pl.pallas_call(gram_kernel, grid=(steps,), in_specs=[pl.BlockSpec((sender...  1.96 us
    pallas_call x3, Pallas kernels, own_part(): pl.pallas_call(own_kernel if e is None else own_fold_kernel, grid=(1,), i...  1.5 us
    ppermute x4, starting transfers between devices, from_partner(): lax.ppermute(block, axis, [(at, at ^ 1 << apart) for at in range(count)])  1.4 us
  transfers between devices with their start and end apart: 4, of which 3 were waited for; matrix products, arithmetic and copies ran while one was open for 0% of the time, Pallas kernels for 6%

profile of v3, /device:TPU:0, one launch (start us, length us, event | category | flops | bytes accessed | tf_op | source)
XLA Modules:
  0.0 63.1 jit_solution(5497030066127166390)
XLA Ops:
  0.0 4.9 %trace_blocks.1 = f32[8,16,16,128]{3,2,1,0:T(8,128)S(1)} custom-call(f32[2,256,2048]{2,1,0:T(8,128)} %x_hbm.1, f32[8,128,128]{2,1,0:T(8,128)} %constant.2.clone.table_hbm), custom_call_target="tpu_custom_call" | custom-call | tf_op jit(solution)/shard_map/trace_blocks/pallas_call | solution.py:120
  4.9 0.0 slice-start
  5.0 0.0 copy-start
  5.0 0.0 copy-start.1
  5.0 0.0 slice-start.1
  5.0 30.3 %all_to_all.10.values_ref.after_ref = f32[128,16,128]{2,1,0:T(8,128)S(1)} all-to-all(f32[128,16,128]{2,1,0:T(8,128)S(1)} %hold.3), channel_id=1, replica_groups=mesh['freq'=8,'trace'=16] {'freq','trace'}, dimensions={0} | all-to-all | bytes 2097152 | tf_op jit(solution)/shard_map/all_to_all | solution.py:353
  35.3 0.0 copy-done
  35.3 0.0 copy-done.1
  35.4 0.6 far_part.1
  35.9 0.6 collective-permute-start.3
  36.6 0.0 slice-done
  36.6 0.0 slice-done.1
  36.6 2.0 %gram.1.c_ref = f32[64,256]{1,0:T(8,128)S(1)} custom-call(f32[128,16,128]{2,1,0:T(8,128)S(1)} %all_to_all.10.values_ref.after_ref, f32[256,16,512]{2,1,0:T(8,128)S(1)} %bitcast.2), custom_call_target="tpu_custom_call" | custom-call | tf_op jit(solution)/shard_map/gram/pallas_call | solution.py:194
  38.5 0.1 collective-permute-start
  38.6 0.3 own_part.2
  39.0 0.9 %collective-permute-done.c_ref = f32[64,256]{1,0:T(8,128)S(1)} collective-permute-done((f32[64,256]{1,0:T(8,128)S(1)}, f32[64,256]{1,0:T(8,128)S(1)}, u32[]{:S(2)}, u32[]{:S(2)}) %collective-permute-start) | collective-permute-done | bytes 65568 | tf_op jit(solution)/shard_map/ppermute | solution.py:344
  39.9 0.3 join_part.2.c_ref
  40.2 0.1 collective-permute-start.1
  40.3 0.9 %own_fold_part.1 = (f32[64,256]{1,0:T(8,128)S(1)}, bf16[512,256]{1,0:T(8,128)(2,1)S(1)}, bf16[512,256]{1,0:T(8,128)(2,1)S(1)}, bf16[256,512]{1,0:T(8,128)(2,1)S(1)}, bf16[256,512]{1,0:T(8,128)(2,1)S(1)}) custom-call(f32[64,256]{1,0:T(8,128)S(1)} %join_part.2.c_ref, f32[4,256,1024]{2,1,0:T(8,128)S(1)} %copy-done, f32[256,512]{1,0:T(8,128)S(1)} %copy-done.1, ...), custom_call_target="tpu_custom_call" | custom-call | flops 100000000 | bytes 1000000 | tf_op jit(solution)/shard_map/own_fold_part/pallas_call | solution.py:264
  41.1 3.4 %collective-permute-done.1.c_ref = f32[64,256]{1,0:T(8,128)S(1)} collective-permute-done((f32[64,256]{1,0:T(8,128)S(1)}, f32[64,256]{1,0:T(8,128)S(1)}, u32[]{:S(2)}, u32[]{:S(2)}) %collective-permute-start.1) | collective-permute-done | bytes 65568 | tf_op jit(solution)/shard_map/ppermute | solution.py:344
  44.5 0.3 join_part.3.c_ref
  44.8 0.6 collective-permute-start.2
  45.4 0.3 own_part.3
  45.7 4.9 %collective-permute-done.2.c_ref = f32[64,256]{1,0:T(8,128)S(1)} collective-permute-done((f32[64,256]{1,0:T(8,128)S(1)}, f32[64,256]{1,0:T(8,128)S(1)}, u32[]{:S(2)}, u32[]{:S(2)}) %collective-permute-start.2) | collective-permute-done | bytes 65568 | tf_op jit(solution)/shard_map/ppermute | solution.py:344
  50.6 0.0 collective-permute-done.3.far_ref
  50.6 0.8 %last_part.1 = f32[16,8,128]{2,1,0:T(8,128)S(1)} custom-call(f32[64,256]{1,0:T(8,128)S(1)} %get-tuple-element.22.own_ref, f32[64,256]{1,0:T(8,128)S(1)} %collective-permute-done.2.c_ref, bf16[512,256]{1,0:T(8,128)(2,1)S(1)} %get-tuple-element.23.high_ref, bf16[512,256]{1,0:T(8,128)(2,1)S(1)} %get-tuple-element.24.low_ref, ...), custom_call_target="tpu_custom_call" | custom-call | tf_op jit(solution)/shard_map/last_part/pallas_call | solution.py:311
  51.4 10.9 %all_to_all.11.x_ref = f32[16,8,128]{2,1,0:T(8,128)S(1)} all-to-all(f32[16,8,128]{2,1,0:T(8,128)S(1)} %last_part.1), channel_id=1, replica_groups={{0,8,16,24,32,40,48,56,64,72,80,88,96,104,112,120},{1,9,17,25,33,41,49,..., dimensions={0} | all-to-all | bytes 131072 | tf_op jit(solution)/shard_map/all_to_all | solution.py:371
  62.4 0.8 %final_part.1 = f32[32,256]{1,0:T(8,128)} custom-call(f32[16,8,128]{2,1,0:T(8,128)S(1)} %all_to_all.11.x_ref), custom_call_target="tpu_custom_call" | custom-call | tf_op jit(solution)/shard_map/final_part/pallas_call | solution.py:334
  (3 shorter events, 0.0 us)
Async XLA Ops:
  4.9 31.6 %slice-start = ((s8[8388608]{0:T(1024)(128)(4,1)}), s8[4194304]{0:T(1024)(128)(4,1)S(1)}, s32[]{:S(2)}) async-start(s8[8388608]{0:T(1024)(128)(4,1)} %bitcast.1), calls=%async_computation.2 | async-start | bytes 8388608
  5.0 30.4 %copy-start = (f32[4,256,1024]{2,1,0:T(8,128)S(1)}, f32[4,256,1024]{2,1,0:T(8,128)}, u32[]{:S(2)}) copy-start(f32[4,256,1024]{2,1,0:T(8,128)} %w_ref.7) | copy-start | bytes 12582916
  5.0 30.4 %copy-start.1 = (f32[256,512]{1,0:T(8,128)S(1)}, f32[256,512]{1,0:T(8,128)}, u32[]{:S(2)}) copy-start(f32[256,512]{1,0:T(8,128)} %e_ref.3) | copy-start | bytes 1572868
  5.0 31.6 %slice-start.1 = ((s8[8388608]{0:T(1024)(128)(4,1)}), s8[4194304]{0:T(1024)(128)(4,1)S(1)}, s32[]{:S(2)}) async-start(s8[8388608]{0:T(1024)(128)(4,1)} %bitcast.1), calls=%async_computation.3 | async-start | bytes 8388608
  35.9 14.7 %collective-permute-start.3 = (f32[256,512]{1,0:T(8,128)S(1)}, f32[256,512]{1,0:T(8,128)S(1)}, u32[]{:S(2)}, u32[]{:S(2)}) collective-permute-start(f32[256,512]{1,0:T(8,128)S(1)} %far_part.1), channel_id=1, source_target_pairs={{0,8},{1,9},{2,10},{3,11},{4,12},{5,13},{6,14},{7,15},{8,0},{9,1},... | collective-permute-start | bytes 1572872 | tf_op jit(solution)/shard_map/ppermute | solution.py:344
  38.5 1.3 %collective-permute-start = (f32[64,256]{1,0:T(8,128)S(1)}, f32[64,256]{1,0:T(8,128)S(1)}, u32[]{:S(2)}, u32[]{:S(2)}) collective-permute-start(f32[64,256]{1,0:T(8,128)S(1)} %gram.1.c_ref), channel_id=1, source_target_pairs={{0,1},{1,0},{2,3},{3,2},{4,5},{5,4},{6,7},{7,6},{8,9},{9,8},{10,11... | collective-permute-start | bytes 196616 | tf_op jit(solution)/shard_map/ppermute | solution.py:344
  40.2 4.3 %collective-permute-start.1 = (f32[64,256]{1,0:T(8,128)S(1)}, f32[64,256]{1,0:T(8,128)S(1)}, u32[]{:S(2)}, u32[]{:S(2)}) collective-permute-start(f32[64,256]{1,0:T(8,128)S(1)} %join_part.2.c_ref), channel_id=1, source_target_pairs={{0,2},{1,3},{2,0},{3,1},{4,6},{5,7},{6,4},{7,5},{8,10},{9,11},{10,... | collective-permute-start | bytes 196616 | tf_op jit(solution)/shard_map/ppermute | solution.py:344
  44.8 5.8 %collective-permute-start.2 = (f32[64,256]{1,0:T(8,128)S(1)}, f32[64,256]{1,0:T(8,128)S(1)}, u32[]{:S(2)}, u32[]{:S(2)}) collective-permute-start(f32[64,256]{1,0:T(8,128)S(1)} %join_part.3.c_ref), channel_id=1, source_target_pairs={{0,4},{1,5},{2,6},{3,7},{4,0},{5,1},{6,2},{7,3},{8,12},{9,13},{10,... | collective-permute-start | bytes 196616 | tf_op jit(solution)/shard_map/ppermute | solution.py:344

commit v4 on v3

--- a/solution.py
+++ b/solution.py
@@ -58,9 +58,9 @@
     return result
 
 
-def trace_kernel(scale, x_hbm, table_hbm, out_ref, x_ref, table_ref, full_ref, x_sem, table_sem):
+def trace_kernel(scale, x_hbm, table_hbm, out_ref, x_ref, table_ref, high_ref, low_ref, x_sem, table_sem):
     shots, offsets, samples = x_hbm.shape
-    count, wide, _ = full_ref.shape
+    count, wide, _ = high_ref.shape
     rows = shots * offsets
     copies = [
         pltpu.make_async_copy(x_hbm.at[s], x_ref.at[pl.ds(s * offsets, offsets)], x_sem.at[s])
@@ -72,38 +72,52 @@
         copy.start()
     lane = lax.broadcasted_iota(jnp.int32, (wide, 128), 1)
     row = lax.broadcasted_iota(jnp.int32, (wide, 128), 0)
-    step = samples // (4 * TAUS)
-    pick = jnp.where(row == step * lane_tau(lane), 1.0, 0.0).astype(BF16)
-    full_ref[...] = jnp.zeros_like(full_ref)
+    pick = jnp.where(row // 2 == lane_tau(lane), 1.0, 0.0).astype(BF16)
     table_copy.wait()
+    even_rows, odd_rows = pl.ds(0, wide // 2, 2), pl.ds(1, wide // 2, 2)
     for d in range(count):
-        full_ref[d, pl.ds(1, wide // 2, 2), :] = table_ref[d]
-    table = [split(full_ref[d]) for d in range(count)]
-    right = [
-        jnp.concatenate(
+        table = table_ref[d]
+        high = table.astype(BF16).astype(F32)
+        high_ref[d, even_rows, :] = high
+        high_ref[d, odd_rows, :] = high
+        low_ref[d, odd_rows, :] = table - high
+        low_ref[(d + count // 2) % count, even_rows, :] = table - high
+
+    def right(ref, blocks):
+        part = [ref[d].astype(BF16) for d in range(count)]
+        return jnp.concatenate(
             [
-                jnp.concatenate([table[-at % count][part], table[(1 - at) % count][part]], axis=1)
-                for at in range(count)
+                jnp.concatenate([part[-at % count], part[(1 - at) % count]], axis=1)
+                for at in range(blocks)
             ],
             axis=0,
         )
-        for part in range(2)
-    ]
+
+    high_table, low_table = right(high_ref, count), right(low_ref, count // 2)
     for copy in copies:
         copy.wait()
-    x = x_ref[...]
-    total = x[:, :128]
-    for at in range(128, samples, 128):
-        total = total + x[:, at : at + 128]
-    pair = split(x)
-    imag = mm3(pair, right, NN)
-    odd = lax.broadcasted_iota(jnp.int32, total.shape, 1) % 2 == 1
+    tiles = range(0, samples, 128)
+    odd = lax.broadcasted_iota(jnp.int32, (rows, 128), 1) % 2 == 1
+    total, high, low = None, [], []
+    for at in tiles:
+        x = x_ref[:, at : at + 128]
+        total = x if total is None else total + x
+        pair = split(x)
+        high.append(pair[0])
+        low.append(pair[1])
+    mix = lambda on_odd, on_even, by: jnp.concatenate(
+        [jnp.where(odd, o, pltpu.roll(e, by, 1)) for o, e in zip(on_odd, on_even)], axis=1
+    )
+    middle = len(high) // 2
+    imag = mm(mix(high, low, 127), high_table, NN) + mm(
+        mix(high[:middle], high[middle:], 127), low_table, NN
+    )
     mean = jnp.sum(jnp.where(odd, total, 0.0), axis=1, keepdims=True) * scale
     real = []
-    for half in range(2):
-        part = slice(half * wide, half * wide + wide)
-        both = mm(jnp.concatenate([p[:, part] for p in pair], axis=0), pick, NN)
-        real.append((both[:rows] + both[rows:]) * (FREQS * scale) + mean)
+    for at in range(2):
+        part = slice(at * wide // 128, (at + 1) * wide // 128)
+        both = [jnp.where(odd, pltpu.roll(e, 1, 1), o) for o, e in zip(high[part], low[part])]
+        real.append(mm(jnp.concatenate(both, axis=1), pick, NN) * (FREQS * scale) + mean)
     parts = []
     for s in range(shots):
         own = slice(s * offsets, s * offsets + offsets)
@@ -127,6 +141,7 @@
         scratch_shapes=[
             pltpu.VMEM((shots * offsets, samples), F32),
             pltpu.VMEM(table.shape, F32),
+            pltpu.VMEM((samples // wide, wide, 128), F32),
             pltpu.VMEM((samples // wide, wide, 128), F32),
             pltpu.SemaphoreType.DMA((shots,)),
             pltpu.SemaphoreType.DMA,
@@ -190,7 +205,7 @@
 def gram(values, sources):
     senders, box, lanes = values.shape
     shots, _, width = sources.shape
-    steps = 2
+    steps = 1
     return pl.pallas_call(
         gram_kernel,
         grid=(steps,),

time: 63.3 us -> 62.6 us (0.989)
  Pallas kernels: 11.1 us -> 10.4 us
where the time goes in v4:
time: 62.6 us; the launch traced here: 62.5 us
  blocking collectives  41.2 us (66%)
  Pallas kernels  10.4 us (17%)
  waiting for transfers between devices  9.22 us (15%)
  starting transfers between devices  1.39 us (2%)
    all_to_all x1, blocking collectives, body(): lax.all_to_all(blocks, ('freq', 'trace'), split_axis=0, concat_axis=0, ti...  30.3 us
    all_to_all x1, blocking collectives, body(): lax.all_to_all(out, ('freq', 'trace'), 0, 0, axis_index_groups=groups, ti...  10.9 us
    ppermute x4, waiting for transfers between devices, from_partner(): lax.ppermute(block, axis, [(at, at ^ 1 << apart) for at in range(count)])  9.22 us
    pallas_call x1, Pallas kernels, trace_blocks(): pl.pallas_call(functools.partial(trace_kernel, scale), in_specs=[pl.Block...  4.56 us
    pallas_call x1, Pallas kernels, gram(): pl.pallas_call(gram_kernel, grid=(steps,), in_specs=[pl.BlockSpec((sender...  1.65 us
    pallas_call x3, Pallas kernels, own_part(): pl.pallas_call(own_kernel if e is None else own_fold_kernel, grid=(1,), i...  1.5 us
    ppermute x4, starting transfers between devices, from_partner(): lax.ppermute(block, axis, [(at, at ^ 1 << apart) for at in range(count)])  1.39 us
  transfers between devices with their start and end apart: 4, of which 3 were waited for; matrix products, arithmetic and copies ran while one was open for 0% of the time, Pallas kernels for 6%

profile of v4, /device:TPU:0, one launch (start us, length us, event | category | flops | bytes accessed | tf_op | source)
XLA Modules:
  0.0 62.5 jit_solution(5808598401381059371)
XLA Ops:
  0.0 4.6 %trace_blocks.1 = f32[8,16,16,128]{3,2,1,0:T(8,128)S(1)} custom-call(f32[2,256,2048]{2,1,0:T(8,128)} %x_hbm.1, f32[8,128,128]{2,1,0:T(8,128)} %constant.2.clone.table_hbm), custom_call_target="tpu_custom_call" | custom-call | tf_op jit(solution)/shard_map/trace_blocks/pallas_call | solution.py:134
  4.6 0.0 slice-start
  4.6 0.0 copy-start
  4.6 0.0 copy-start.1
  4.6 0.0 slice-start.1
  4.6 30.3 %all_to_all.10.values_ref.after_ref = f32[128,16,128]{2,1,0:T(8,128)S(1)} all-to-all(f32[128,16,128]{2,1,0:T(8,128)S(1)} %hold.3), channel_id=1, replica_groups=mesh['freq'=8,'trace'=16] {'freq','trace'}, dimensions={0} | all-to-all | bytes 2097152 | tf_op jit(solution)/shard_map/all_to_all | solution.py:368
  35.0 0.0 copy-done
  35.0 0.0 copy-done.1
  35.0 0.6 far_part.1
  35.6 0.6 collective-permute-start.3
  36.2 0.0 slice-done
  36.2 0.0 slice-done.1
  36.2 1.7 %gram.1.c_ref = f32[64,256]{1,0:T(8,128)S(1)} custom-call(f32[128,16,128]{2,1,0:T(8,128)S(1)} %all_to_all.10.values_ref.after_ref, f32[256,16,512]{2,1,0:T(8,128)S(1)} %bitcast.2), custom_call_target="tpu_custom_call" | custom-call | tf_op jit(solution)/shard_map/gram/pallas_call | solution.py:209
  37.9 0.1 collective-permute-start
  37.9 0.3 own_part.2
  38.3 0.9 %collective-permute-done.c_ref = f32[64,256]{1,0:T(8,128)S(1)} collective-permute-done((f32[64,256]{1,0:T(8,128)S(1)}, f32[64,256]{1,0:T(8,128)S(1)}, u32[]{:S(2)}, u32[]{:S(2)}) %collective-permute-start) | collective-permute-done | bytes 65568 | tf_op jit(solution)/shard_map/ppermute | solution.py:359
  39.2 0.3 join_part.2.c_ref
  39.5 0.1 collective-permute-start.1
  39.6 0.9 %own_fold_part.1 = (f32[64,256]{1,0:T(8,128)S(1)}, bf16[512,256]{1,0:T(8,128)(2,1)S(1)}, bf16[512,256]{1,0:T(8,128)(2,1)S(1)}, bf16[256,512]{1,0:T(8,128)(2,1)S(1)}, bf16[256,512]{1,0:T(8,128)(2,1)S(1)}) custom-call(f32[64,256]{1,0:T(8,128)S(1)} %join_part.2.c_ref, f32[4,256,1024]{2,1,0:T(8,128)S(1)} %copy-done, f32[256,512]{1,0:T(8,128)S(1)} %copy-done.1, ...), custom_call_target="tpu_custom_call" | custom-call | flops 100000000 | bytes 1000000 | tf_op jit(solution)/shard_map/own_fold_part/pallas_call | solution.py:279
  40.4 3.4 %collective-permute-done.1.c_ref = f32[64,256]{1,0:T(8,128)S(1)} collective-permute-done((f32[64,256]{1,0:T(8,128)S(1)}, f32[64,256]{1,0:T(8,128)S(1)}, u32[]{:S(2)}, u32[]{:S(2)}) %collective-permute-start.1) | collective-permute-done | bytes 65568 | tf_op jit(solution)/shard_map/ppermute | solution.py:359
  43.8 0.3 join_part.3.c_ref
  44.1 0.6 collective-permute-start.2
  44.7 0.3 own_part.3
  45.0 4.9 %collective-permute-done.2.c_ref = f32[64,256]{1,0:T(8,128)S(1)} collective-permute-done((f32[64,256]{1,0:T(8,128)S(1)}, f32[64,256]{1,0:T(8,128)S(1)}, u32[]{:S(2)}, u32[]{:S(2)}) %collective-permute-start.2) | collective-permute-done | bytes 65568 | tf_op jit(solution)/shard_map/ppermute | solution.py:359
  50.0 0.0 collective-permute-done.3.far_ref
  50.0 0.8 %last_part.1 = f32[16,8,128]{2,1,0:T(8,128)S(1)} custom-call(f32[64,256]{1,0:T(8,128)S(1)} %get-tuple-element.22.own_ref, f32[64,256]{1,0:T(8,128)S(1)} %collective-permute-done.2.c_ref, bf16[512,256]{1,0:T(8,128)(2,1)S(1)} %get-tuple-element.23.high_ref, bf16[512,256]{1,0:T(8,128)(2,1)S(1)} %get-tuple-element.24.low_ref, ...), custom_call_target="tpu_custom_call" | custom-call | tf_op jit(solution)/shard_map/last_part/pallas_call | solution.py:326
  50.8 10.9 %all_to_all.11.x_ref = f32[16,8,128]{2,1,0:T(8,128)S(1)} all-to-all(f32[16,8,128]{2,1,0:T(8,128)S(1)} %last_part.1), channel_id=1, replica_groups={{0,8,16,24,32,40,48,56,64,72,80,88,96,104,112,120},{1,9,17,25,33,41,49,..., dimensions={0} | all-to-all | bytes 131072 | tf_op jit(solution)/shard_map/all_to_all | solution.py:386
  61.7 0.8 %final_part.1 = f32[32,256]{1,0:T(8,128)} custom-call(f32[16,8,128]{2,1,0:T(8,128)S(1)} %all_to_all.11.x_ref), custom_call_target="tpu_custom_call" | custom-call | tf_op jit(solution)/shard_map/final_part/pallas_call | solution.py:349
  (3 shorter events, 0.0 us)
Async XLA Ops:
  4.6 31.6 %slice-start = ((s8[8388608]{0:T(1024)(128)(4,1)}), s8[4194304]{0:T(1024)(128)(4,1)S(1)}, s32[]{:S(2)}) async-start(s8[8388608]{0:T(1024)(128)(4,1)} %bitcast.1), calls=%async_computation.2 | async-start | bytes 8388608
  4.6 30.4 %copy-start = (f32[4,256,1024]{2,1,0:T(8,128)S(1)}, f32[4,256,1024]{2,1,0:T(8,128)}, u32[]{:S(2)}) copy-start(f32[4,256,1024]{2,1,0:T(8,128)} %w_ref.7) | copy-start | bytes 12582916
  4.6 30.4 %copy-start.1 = (f32[256,512]{1,0:T(8,128)S(1)}, f32[256,512]{1,0:T(8,128)}, u32[]{:S(2)}) copy-start(f32[256,512]{1,0:T(8,128)} %e_ref.3) | copy-start | bytes 1572868
  4.6 31.6 %slice-start.1 = ((s8[8388608]{0:T(1024)(128)(4,1)}), s8[4194304]{0:T(1024)(128)(4,1)S(1)}, s32[]{:S(2)}) async-start(s8[8388608]{0:T(1024)(128)(4,1)} %bitcast.1), calls=%async_computation.3 | async-start | bytes 8388608
  35.6 14.4 %collective-permute-start.3 = (f32[256,512]{1,0:T(8,128)S(1)}, f32[256,512]{1,0:T(8,128)S(1)}, u32[]{:S(2)}, u32[]{:S(2)}) collective-permute-start(f32[256,512]{1,0:T(8,128)S(1)} %far_part.1), channel_id=1, source_target_pairs={{0,8},{1,9},{2,10},{3,11},{4,12},{5,13},{6,14},{7,15},{8,0},{9,1},... | collective-permute-start | bytes 1572872 | tf_op jit(solution)/shard_map/ppermute | solution.py:359
  37.9 1.3 %collective-permute-start = (f32[64,256]{1,0:T(8,128)S(1)}, f32[64,256]{1,0:T(8,128)S(1)}, u32[]{:S(2)}, u32[]{:S(2)}) collective-permute-start(f32[64,256]{1,0:T(8,128)S(1)} %gram.1.c_ref), channel_id=1, source_target_pairs={{0,1},{1,0},{2,3},{3,2},{4,5},{5,4},{6,7},{7,6},{8,9},{9,8},{10,11... | collective-permute-start | bytes 196616 | tf_op jit(solution)/shard_map/ppermute | solution.py:359
  39.5 4.3 %collective-permute-start.1 = (f32[64,256]{1,0:T(8,128)S(1)}, f32[64,256]{1,0:T(8,128)S(1)}, u32[]{:S(2)}, u32[]{:S(2)}) collective-permute-start(f32[64,256]{1,0:T(8,128)S(1)} %join_part.2.c_ref), channel_id=1, source_target_pairs={{0,2},{1,3},{2,0},{3,1},{4,6},{5,7},{6,4},{7,5},{8,10},{9,11},{10,... | collective-permute-start | bytes 196616 | tf_op jit(solution)/shard_map/ppermute | solution.py:359
  44.1 5.8 %collective-permute-start.2 = (f32[64,256]{1,0:T(8,128)S(1)}, f32[64,256]{1,0:T(8,128)S(1)}, u32[]{:S(2)}, u32[]{:S(2)}) collective-permute-start(f32[64,256]{1,0:T(8,128)S(1)} %join_part.3.c_ref), channel_id=1, source_target_pairs={{0,4},{1,5},{2,6},{3,7},{4,0},{5,1},{6,2},{7,3},{8,12},{9,13},{10,... | collective-permute-start | bytes 196616 | tf_op jit(solution)/shard_map/ppermute | solution.py:359

commit v5 on v4

--- a/solution.py
+++ b/solution.py
@@ -258,14 +258,15 @@
     weights = w_ref[0]
     own = split(jnp.concatenate([weights[:, :k], weights[:, 2 * k : 3 * k]], axis=0))
     own_ref[...] = turn(mm3(split(c_ref[...]), own, NT))
-    high, low = split(jnp.concatenate([weights[:, k : 2 * k], weights[:, 3 * k :]], axis=0))
+    partner = jnp.concatenate([weights[:, k : 2 * k], weights[:, 3 * k :]], axis=0)
+    high, low = split(partner.T)
     high_ref[...] = high
     low_ref[...] = low
 
 
 def own_fold_kernel(c_ref, w_ref, e_ref, last_ref, own_ref, high_ref, low_ref, *fold_refs):
     own_kernel(c_ref, w_ref, own_ref, high_ref, low_ref)
-    for ref, part in zip(fold_refs, split(fold(e_ref[...], last_ref[0], 0))):
+    for ref, part in zip(fold_refs, split(fold(e_ref[...], last_ref[0], 0).T)):
         ref[...] = part
 
 
@@ -275,7 +276,7 @@
     whole = lambda *shape: pl.BlockSpec(shape, lambda i: (0,) * len(shape))
     sheet = lambda at: pl.BlockSpec((1, k, 4 * k), lambda i: (at, 0, 0))
     extra = () if e is None else (e, weights)
-    pairs = [(2 * k, k)] * 2 + ([] if e is None else [e.shape] * 2)
+    pairs = [(k, 2 * k)] * 2 + ([] if e is None else [e.shape[::-1]] * 2)
     return pl.pallas_call(
         own_kernel if e is None else own_fold_kernel,
         grid=(1,),
@@ -291,7 +292,7 @@
 
 
 def joined(own_ref, c_ref, high_ref, low_ref):
-    return own_ref[...] + turn(mm3(split(c_ref[...]), (high_ref[...], low_ref[...]), NT))
+    return own_ref[...] + turn(mm3(split(c_ref[...]), (high_ref[...], low_ref[...]), NN))
 
 
 def join_kernel(own_ref, c_ref, high_ref, low_ref, out_ref):
@@ -305,7 +306,7 @@
     side = lax.axis_index("trace") // 8
     pairs = [(near_high[...], near_low[...]), split(far_ref[...])]
     for at, pair in enumerate(pairs):
-        values = mm3(row, pair, NT)
+        values = mm3(row, pair, NT if at else NN)
         for tile in range(values.shape[1] // 128):
             lanes = slice(128 * tile, 128 * tile + 128)
             parts = [values[8 * g : 8 * g + 8, lanes] for g in range(4)]

time: 62.6 us -> 62.4 us (level)
  no operation moved by 1% of the time
where the time goes in v5:
time: 62.4 us; the launch traced here: 62.3 us
  blocking collectives  41.2 us (66%)
  Pallas kernels  10.3 us (17%)
  waiting for transfers between devices  9.27 us (15%)
  starting transfers between devices  1.39 us (2%)
    all_to_all x1, blocking collectives, body(): lax.all_to_all(blocks, ('freq', 'trace'), split_axis=0, concat_axis=0, ti...  30.3 us
    all_to_all x1, blocking collectives, body(): lax.all_to_all(out, ('freq', 'trace'), 0, 0, axis_index_groups=groups, ti...  10.9 us
    ppermute x4, waiting for transfers between devices, from_partner(): lax.ppermute(block, axis, [(at, at ^ 1 << apart) for at in range(count)])  9.27 us
    pallas_call x1, Pallas kernels, trace_blocks(): pl.pallas_call(functools.partial(trace_kernel, scale), in_specs=[pl.Block...  4.56 us
    pallas_call x1, Pallas kernels, gram(): pl.pallas_call(gram_kernel, grid=(steps,), in_specs=[pl.BlockSpec((sender...  1.66 us
    pallas_call x3, Pallas kernels, own_part(): pl.pallas_call(own_kernel if e is None else own_fold_kernel, grid=(1,), i...  1.47 us
    ppermute x4, starting transfers between devices, from_partner(): lax.ppermute(block, axis, [(at, at ^ 1 << apart) for at in range(count)])  1.39 us
  transfers between devices with their start and end apart: 4, of which 3 were waited for; matrix products, arithmetic and copies ran while one was open for 0% of the time, Pallas kernels for 6%

profile of v5, /device:TPU:0, one launch (start us, length us, event | category | flops | bytes accessed | tf_op | source)
XLA Modules:
  0.0 62.3 jit_solution(12047909523182324755)
XLA Ops:
  0.0 4.6 %trace_blocks.1 = f32[8,16,16,128]{3,2,1,0:T(8,128)S(1)} custom-call(f32[2,256,2048]{2,1,0:T(8,128)} %x_hbm.1, f32[8,128,128]{2,1,0:T(8,128)} %constant.2.clone.table_hbm), custom_call_target="tpu_custom_call" | custom-call | tf_op jit(solution)/shard_map/trace_blocks/pallas_call | solution.py:134
  4.6 0.0 slice-start
  4.6 0.0 copy-start
  4.6 0.0 copy-start.1
  4.6 0.0 slice-start.1
  4.6 30.3 %all_to_all.10.values_ref.after_ref = f32[128,16,128]{2,1,0:T(8,128)S(1)} all-to-all(f32[128,16,128]{2,1,0:T(8,128)S(1)} %hold.3), channel_id=1, replica_groups=mesh['freq'=8,'trace'=16] {'freq','trace'}, dimensions={0} | all-to-all | bytes 2097152 | tf_op jit(solution)/shard_map/all_to_all | solution.py:369
  35.0 0.0 copy-done
  35.0 0.0 copy-done.1
  35.0 0.6 far_part.1
  35.6 0.6 collective-permute-start.3
  36.2 0.0 slice-done
  36.2 0.0 slice-done.1
  36.2 1.7 %gram.1.c_ref = f32[64,256]{1,0:T(8,128)S(1)} custom-call(f32[128,16,128]{2,1,0:T(8,128)S(1)} %all_to_all.10.values_ref.after_ref, f32[256,16,512]{2,1,0:T(8,128)S(1)} %bitcast.2), custom_call_target="tpu_custom_call" | custom-call | tf_op jit(solution)/shard_map/gram/pallas_call | solution.py:209
  37.9 0.1 collective-permute-start
  37.9 0.3 own_part.2
  38.2 0.9 %collective-permute-done.c_ref = f32[64,256]{1,0:T(8,128)S(1)} collective-permute-done((f32[64,256]{1,0:T(8,128)S(1)}, f32[64,256]{1,0:T(8,128)S(1)}, u32[]{:S(2)}, u32[]{:S(2)}) %collective-permute-start) | collective-permute-done | bytes 65568 | tf_op jit(solution)/shard_map/ppermute | solution.py:360
  39.2 0.2 join_part.2.c_ref
  39.4 0.1 collective-permute-start.1
  39.5 0.9 %own_fold_part.1 = (f32[64,256]{1,0:T(8,128)S(1)}, bf16[256,512]{1,0:T(8,128)(2,1)S(1)}, bf16[256,512]{1,0:T(8,128)(2,1)S(1)}, bf16[512,256]{1,0:T(8,128)(2,1)S(1)}, bf16[512,256]{1,0:T(8,128)(2,1)S(1)}) custom-call(f32[64,256]{1,0:T(8,128)S(1)} %join_part.2.c_ref, f32[4,256,1024]{2,1,0:T(8,128)S(1)} %copy-done, f32[256,512]{1,0:T(8,128)S(1)} %copy-done.1, ...), custom_call_target="tpu_custom_call" | custom-call | flops 100000000 | bytes 1000000 | tf_op jit(solution)/shard_map/own_fold_part/pallas_call | solution.py:280
  40.4 3.4 %collective-permute-done.1.c_ref = f32[64,256]{1,0:T(8,128)S(1)} collective-permute-done((f32[64,256]{1,0:T(8,128)S(1)}, f32[64,256]{1,0:T(8,128)S(1)}, u32[]{:S(2)}, u32[]{:S(2)}) %collective-permute-start.1) | collective-permute-done | bytes 65568 | tf_op jit(solution)/shard_map/ppermute | solution.py:360
  43.8 0.2 join_part.3.c_ref
  44.0 0.6 collective-permute-start.2
  44.6 0.3 own_part.3
  44.9 5.0 %collective-permute-done.2.c_ref = f32[64,256]{1,0:T(8,128)S(1)} collective-permute-done((f32[64,256]{1,0:T(8,128)S(1)}, f32[64,256]{1,0:T(8,128)S(1)}, u32[]{:S(2)}, u32[]{:S(2)}) %collective-permute-start.2) | collective-permute-done | bytes 65568 | tf_op jit(solution)/shard_map/ppermute | solution.py:360
  49.8 0.0 collective-permute-done.3.far_ref
  49.8 0.8 %last_part.1 = f32[16,8,128]{2,1,0:T(8,128)S(1)} custom-call(f32[64,256]{1,0:T(8,128)S(1)} %get-tuple-element.22.own_ref, f32[64,256]{1,0:T(8,128)S(1)} %collective-permute-done.2.c_ref, bf16[256,512]{1,0:T(8,128)(2,1)S(1)} %get-tuple-element.23.high_ref, bf16[256,512]{1,0:T(8,128)(2,1)S(1)} %get-tuple-element.24.low_ref, ...), custom_call_target="tpu_custom_call" | custom-call | tf_op jit(solution)/shard_map/last_part/pallas_call | solution.py:327
  50.6 10.9 %all_to_all.11.x_ref = f32[16,8,128]{2,1,0:T(8,128)S(1)} all-to-all(f32[16,8,128]{2,1,0:T(8,128)S(1)} %last_part.1), channel_id=1, replica_groups={{0,8,16,24,32,40,48,56,64,72,80,88,96,104,112,120},{1,9,17,25,33,41,49,..., dimensions={0} | all-to-all | bytes 131072 | tf_op jit(solution)/shard_map/all_to_all | solution.py:387
  61.5 0.8 %final_part.1 = f32[32,256]{1,0:T(8,128)} custom-call(f32[16,8,128]{2,1,0:T(8,128)S(1)} %all_to_all.11.x_ref), custom_call_target="tpu_custom_call" | custom-call | tf_op jit(solution)/shard_map/final_part/pallas_call | solution.py:350
  (3 shorter events, 0.0 us)
Async XLA Ops:
  4.6 31.6 %slice-start = ((s8[8388608]{0:T(1024)(128)(4,1)}), s8[4194304]{0:T(1024)(128)(4,1)S(1)}, s32[]{:S(2)}) async-start(s8[8388608]{0:T(1024)(128)(4,1)} %bitcast.1), calls=%async_computation.2 | async-start | bytes 8388608
  4.6 30.4 %copy-start = (f32[4,256,1024]{2,1,0:T(8,128)S(1)}, f32[4,256,1024]{2,1,0:T(8,128)}, u32[]{:S(2)}) copy-start(f32[4,256,1024]{2,1,0:T(8,128)} %w_ref.7) | copy-start | bytes 12582916
  4.6 30.4 %copy-start.1 = (f32[256,512]{1,0:T(8,128)S(1)}, f32[256,512]{1,0:T(8,128)}, u32[]{:S(2)}) copy-start(f32[256,512]{1,0:T(8,128)} %e_ref.3) | copy-start | bytes 1572868
  4.6 31.6 %slice-start.1 = ((s8[8388608]{0:T(1024)(128)(4,1)}), s8[4194304]{0:T(1024)(128)(4,1)S(1)}, s32[]{:S(2)}) async-start(s8[8388608]{0:T(1024)(128)(4,1)} %bitcast.1), calls=%async_computation.3 | async-start | bytes 8388608
  35.6 14.3 %collective-permute-start.3 = (f32[256,512]{1,0:T(8,128)S(1)}, f32[256,512]{1,0:T(8,128)S(1)}, u32[]{:S(2)}, u32[]{:S(2)}) collective-permute-start(f32[256,512]{1,0:T(8,128)S(1)} %far_part.1), channel_id=1, source_target_pairs={{0,8},{1,9},{2,10},{3,11},{4,12},{5,13},{6,14},{7,15},{8,0},{9,1},... | collective-permute-start | bytes 1572872 | tf_op jit(solution)/shard_map/ppermute | solution.py:360
  37.9 1.3 %collective-permute-start = (f32[64,256]{1,0:T(8,128)S(1)}, f32[64,256]{1,0:T(8,128)S(1)}, u32[]{:S(2)}, u32[]{:S(2)}) collective-permute-start(f32[64,256]{1,0:T(8,128)S(1)} %gram.1.c_ref), channel_id=1, source_target_pairs={{0,1},{1,0},{2,3},{3,2},{4,5},{5,4},{6,7},{7,6},{8,9},{9,8},{10,11... | collective-permute-start | bytes 196616 | tf_op jit(solution)/shard_map/ppermute | solution.py:360
  39.4 4.3 %collective-permute-start.1 = (f32[64,256]{1,0:T(8,128)S(1)}, f32[64,256]{1,0:T(8,128)S(1)}, u32[]{:S(2)}, u32[]{:S(2)}) collective-permute-start(f32[64,256]{1,0:T(8,128)S(1)} %join_part.2.c_ref), channel_id=1, source_target_pairs={{0,2},{1,3},{2,0},{3,1},{4,6},{5,7},{6,4},{7,5},{8,10},{9,11},{10,... | collective-permute-start | bytes 196616 | tf_op jit(solution)/shard_map/ppermute | solution.py:360
  44.0 5.8 %collective-permute-start.2 = (f32[64,256]{1,0:T(8,128)S(1)}, f32[64,256]{1,0:T(8,128)S(1)}, u32[]{:S(2)}, u32[]{:S(2)}) collective-permute-start(f32[64,256]{1,0:T(8,128)S(1)} %join_part.3.c_ref), channel_id=1, source_target_pairs={{0,4},{1,5},{2,6},{3,7},{4,0},{5,1},{6,2},{7,3},{8,12},{9,13},{10,... | collective-permute-start | bytes 196616 | tf_op jit(solution)/shard_map/ppermute | solution.py:360

commit v6 on v5

--- a/solution.py
+++ b/solution.py
@@ -32,13 +32,9 @@
     return both[:rows] + both[rows:] + mm(a_pair[0], b_pair[1], dims)
 
 
-def lane_tau(lane):
-    return 64 * (lane % 16 // 8) + 8 * (lane // 16) + lane % 8
-
-
 def cot_table(samples, wide, scale):
     step = samples // (4 * TAUS)
-    taus = lane_tau(np.arange(128))
+    taus = np.arange(128)
     gap = wide * np.arange(samples // wide)[:, None, None] + step * taus
     gap = gap - (2 * np.arange(wide // 2)[None, :, None] + 1)
     return (scale / np.tan(np.pi * gap / samples)).astype(np.float32)
@@ -72,7 +68,7 @@
         copy.start()
     lane = lax.broadcasted_iota(jnp.int32, (wide, 128), 1)
     row = lax.broadcasted_iota(jnp.int32, (wide, 128), 0)
-    pick = jnp.where(row // 2 == lane_tau(lane), 1.0, 0.0).astype(BF16)
+    pick = jnp.where(row // 2 == lane, 1.0, 0.0).astype(BF16)
     table_copy.wait()
     even_rows, odd_rows = pl.ds(0, wide // 2, 2), pl.ds(1, wide // 2, 2)
     for d in range(count):
@@ -118,12 +114,14 @@
         part = slice(at * wide // 128, (at + 1) * wide // 128)
         both = [jnp.where(odd, pltpu.roll(e, 1, 1), o) for o, e in zip(high[part], low[part])]
         real.append(mm(jnp.concatenate(both, axis=1), pick, NN) * (FREQS * scale) + mean)
-    parts = []
-    for s in range(shots):
-        own = slice(s * offsets, s * offsets + offsets)
-        parts += [real[0][own], real[1][own], imag[own, :128], imag[own, 128:]]
-    for r, block in enumerate(move_groups(parts, 16)):
-        out_ref[r] = block.reshape(out_ref.shape[1:])
+    for half in range(2):
+        lanes = slice(128 * half, 128 * half + 128)
+        parts = []
+        for s in range(shots):
+            own = slice(s * offsets, s * offsets + offsets)
+            parts += [real[half][own], imag[own, lanes]]
+        for q, block in enumerate(move_groups(parts, 32)):
+            out_ref[4 * half + q] = block.reshape(out_ref.shape[1:])
 
 
 def trace_blocks(traces, freq_count, trace_count):
@@ -266,7 +264,7 @@
 
 def own_fold_kernel(c_ref, w_ref, e_ref, last_ref, own_ref, high_ref, low_ref, *fold_refs):
     own_kernel(c_ref, w_ref, own_ref, high_ref, low_ref)
-    for ref, part in zip(fold_refs, split(fold(e_ref[...], last_ref[0], 0).T)):
+    for ref, part in zip(fold_refs, split(fold(e_ref[...], last_ref[0], 0))):
         ref[...] = part
 
 
@@ -276,7 +274,7 @@
     whole = lambda *shape: pl.BlockSpec(shape, lambda i: (0,) * len(shape))
     sheet = lambda at: pl.BlockSpec((1, k, 4 * k), lambda i: (at, 0, 0))
     extra = () if e is None else (e, weights)
-    pairs = [(k, 2 * k)] * 2 + ([] if e is None else [e.shape[::-1]] * 2)
+    pairs = [(k, 2 * k)] * 2 + ([] if e is None else [e.shape] * 2)
     return pl.pallas_call(
         own_kernel if e is None else own_fold_kernel,
         grid=(1,),
@@ -302,16 +300,15 @@
 def last_kernel(own_ref, c_ref, high_ref, low_ref, near_high, near_low, far_ref, out_ref):
     c = joined(own_ref, c_ref, high_ref, low_ref)
     half = c.shape[0] // 2
-    row = split(jnp.concatenate([c[:half], -c[half:]], axis=1))
+    row = jnp.concatenate(split(jnp.concatenate([c[:half], -c[half:]], axis=1)), axis=0)
     side = lax.axis_index("trace") // 8
     pairs = [(near_high[...], near_low[...]), split(far_ref[...])]
-    for at, pair in enumerate(pairs):
-        values = mm3(row, pair, NT if at else NN)
-        for tile in range(values.shape[1] // 128):
-            lanes = slice(128 * tile, 128 * tile + 128)
-            parts = [values[8 * g : 8 * g + 8, lanes] for g in range(4)]
-            for q, block in enumerate(move_groups(parts, 32)):
-                out_ref[2 * (4 * tile + q) + (at ^ side)] = block
+    for at, (high, low) in enumerate(pairs):
+        both = mm(high, row, NT)
+        values = both[:, :half] + both[:, half:] + mm(low, row[:half], NT)
+        for q in range(values.shape[0] // 32):
+            rows = [values[32 * q + 8 * g : 32 * q + 8 * g + 8] for g in range(4)]
+            out_ref[2 * q + (at ^ side)] = jnp.concatenate(rows, axis=1)
 
 
 def join_part(own, c, high, low):
@@ -335,15 +332,11 @@
 def final_kernel(x_ref, out_ref):
     x = x_ref[...]
     x = x.reshape(x.shape[0] // 2, 2, 8, 128)
-    x = (x[:, 0] + x[:, 1]).reshape(-1, 128)
-    x = jnp.concatenate([x, jnp.zeros_like(x)], axis=0).T
-    low = lax.broadcasted_iota(jnp.int32, (32, 128), 1) < 64
-    for tile in range(2):
-        first = x[64 * tile : 64 * tile + 32]
-        second = x[64 * tile + 32 : 64 * tile + 64]
-        out_ref[:, 128 * tile : 128 * tile + 128] = jnp.where(
-            low, first, pltpu.roll(second, 64, 1)
-        )
+    x = x[:, 0] + x[:, 1]
+    for tile in range(TAUS // 128):
+        parts = [x[4 * tile + q] for q in range(4)]
+        for g, block in enumerate(move_groups(parts, 32)):
+            out_ref[8 * g : 8 * g + 8, 128 * tile : 128 * tile + 128] = block
 
 
 def final_part(x):

time: 62.4 us -> 62.2 us (level)
  no operation moved by 1% of the time
where the time goes in v6:
time: 62.2 us; the launch traced here: 62.1 us
  blocking collectives  41.3 us (66%)
  Pallas kernels  9.89 us (16%)
  waiting for transfers between devices  9.39 us (15%)
  starting transfers between devices  1.39 us (2%)
    all_to_all x1, blocking collectives, body(): lax.all_to_all(blocks, ('freq', 'trace'), split_axis=0, concat_axis=0, ti...  30.3 us
    all_to_all x1, blocking collectives, body(): lax.all_to_all(out, ('freq', 'trace'), 0, 0, axis_index_groups=groups, ti...  10.9 us
    ppermute x4, waiting for transfers between devices, from_partner(): lax.ppermute(block, axis, [(at, at ^ 1 << apart) for at in range(count)])  9.39 us
    pallas_call x1, Pallas kernels, trace_blocks(): pl.pallas_call(functools.partial(trace_kernel, scale), in_specs=[pl.Block...  4.32 us
    pallas_call x1, Pallas kernels, gram(): pl.pallas_call(gram_kernel, grid=(steps,), in_specs=[pl.BlockSpec((sender...  1.66 us
    ppermute x4, starting transfers between devices, from_partner(): lax.ppermute(block, axis, [(at, at ^ 1 << apart) for at in range(count)])  1.39 us
    pallas_call x3, Pallas kernels, own_part(): pl.pallas_call(own_kernel if e is None else own_fold_kernel, grid=(1,), i...  1.34 us
  transfers between devices with their start and end apart: 4, of which 3 were waited for; matrix products, arithmetic and copies ran while one was open for 0% of the time, Pallas kernels for 6%

profile of v6, /device:TPU:0, one launch (start us, length us, event | category | flops | bytes accessed | tf_op | source)
XLA Modules:
  0.0 62.1 jit_solution(6596890609738453932)
XLA Ops:
  0.0 4.3 %trace_blocks.1 = f32[8,16,16,128]{3,2,1,0:T(8,128)S(1)} custom-call(f32[2,256,2048]{2,1,0:T(8,128)} %x_hbm.1, f32[8,128,128]{2,1,0:T(8,128)} %constant.2.clone.table_hbm), custom_call_target="tpu_custom_call" | custom-call | tf_op jit(solution)/shard_map/trace_blocks/pallas_call | solution.py:132
  4.3 0.0 slice-start
  4.3 0.0 copy-start
  4.4 0.0 copy-start.1
  4.4 0.0 slice-start.1
  4.4 30.3 %all_to_all.10.values_ref.after_ref = f32[128,16,128]{2,1,0:T(8,128)S(1)} all-to-all(f32[128,16,128]{2,1,0:T(8,128)S(1)} %hold.3), channel_id=1, replica_groups=mesh['freq'=8,'trace'=16] {'freq','trace'}, dimensions={0} | all-to-all | bytes 2097152 | tf_op jit(solution)/shard_map/all_to_all | solution.py:362
  34.7 0.0 copy-done
  34.7 0.0 copy-done.1
  34.7 0.6 far_part.1
  35.3 0.6 %collective-permute-start.3 = (f32[256,512]{1,0:T(8,128)S(1)}, f32[256,512]{1,0:T(8,128)S(1)}, u32[]{:S(2)}, u32[]{:S(2)}) collective-permute-start(f32[256,512]{1,0:T(8,128)S(1)} %far_part.1), channel_id=1, source_target_pairs={{0,8},{1,9},{2,10},{3,11},{4,12},{5,13},{6,14},{7,15},{8,0},{9,1},... | collective-permute-start | bytes 1572872 | tf_op jit(solution)/shard_map/ppermute | solution.py:353
  35.9 0.0 slice-done
  35.9 0.0 slice-done.1
  35.9 1.7 %gram.1.c_ref = f32[64,256]{1,0:T(8,128)S(1)} custom-call(f32[128,16,128]{2,1,0:T(8,128)S(1)} %all_to_all.10.values_ref.after_ref, f32[256,16,512]{2,1,0:T(8,128)S(1)} %bitcast.2), custom_call_target="tpu_custom_call" | custom-call | tf_op jit(solution)/shard_map/gram/pallas_call | solution.py:207
  37.6 0.1 collective-permute-start
  37.7 0.3 own_part.2
  38.0 0.9 %collective-permute-done.c_ref = f32[64,256]{1,0:T(8,128)S(1)} collective-permute-done((f32[64,256]{1,0:T(8,128)S(1)}, f32[64,256]{1,0:T(8,128)S(1)}, u32[]{:S(2)}, u32[]{:S(2)}) %collective-permute-start) | collective-permute-done | bytes 65568 | tf_op jit(solution)/shard_map/ppermute | solution.py:353
  38.9 0.2 join_part.2.c_ref
  39.2 0.1 collective-permute-start.1
  39.3 0.7 %own_fold_part.1 = (f32[64,256]{1,0:T(8,128)S(1)}, bf16[256,512]{1,0:T(8,128)(2,1)S(1)}, bf16[256,512]{1,0:T(8,128)(2,1)S(1)}, bf16[256,512]{1,0:T(8,128)(2,1)S(1)}, bf16[256,512]{1,0:T(8,128)(2,1)S(1)}) custom-call(f32[64,256]{1,0:T(8,128)S(1)} %join_part.2.c_ref, f32[4,256,1024]{2,1,0:T(8,128)S(1)} %copy-done, f32[256,512]{1,0:T(8,128)S(1)} %copy-done.1, ...), custom_call_target="tpu_custom_call" | custom-call | flops 100000000 | bytes 1000000 | tf_op jit(solution)/shard_map/own_fold_part/pallas_call | solution.py:278
  40.0 3.5 %collective-permute-done.1.c_ref = f32[64,256]{1,0:T(8,128)S(1)} collective-permute-done((f32[64,256]{1,0:T(8,128)S(1)}, f32[64,256]{1,0:T(8,128)S(1)}, u32[]{:S(2)}, u32[]{:S(2)}) %collective-permute-start.1) | collective-permute-done | bytes 65568 | tf_op jit(solution)/shard_map/ppermute | solution.py:353
  43.5 0.2 join_part.3.c_ref
  43.7 0.6 collective-permute-start.2
  44.3 0.3 own_part.3
  44.6 5.0 %collective-permute-done.2.c_ref = f32[64,256]{1,0:T(8,128)S(1)} collective-permute-done((f32[64,256]{1,0:T(8,128)S(1)}, f32[64,256]{1,0:T(8,128)S(1)}, u32[]{:S(2)}, u32[]{:S(2)}) %collective-permute-start.2) | collective-permute-done | bytes 65568 | tf_op jit(solution)/shard_map/ppermute | solution.py:353
  49.6 0.0 collective-permute-done.3.far_ref
  49.6 0.8 %last_part.1 = f32[16,8,128]{2,1,0:T(8,128)S(1)} custom-call(f32[64,256]{1,0:T(8,128)S(1)} %get-tuple-element.22.own_ref, f32[64,256]{1,0:T(8,128)S(1)} %collective-permute-done.2.c_ref, bf16[256,512]{1,0:T(8,128)(2,1)S(1)} %get-tuple-element.23.high_ref, bf16[256,512]{1,0:T(8,128)(2,1)S(1)} %get-tuple-element.24.low_ref, ...), custom_call_target="tpu_custom_call" | custom-call | tf_op jit(solution)/shard_map/last_part/pallas_call | solution.py:324
  50.4 10.9 %all_to_all.11.x_ref = f32[16,8,128]{2,1,0:T(8,128)S(1)} all-to-all(f32[16,8,128]{2,1,0:T(8,128)S(1)} %last_part.1), channel_id=1, replica_groups={{0,8,16,24,32,40,48,56,64,72,80,88,96,104,112,120},{1,9,17,25,33,41,49,..., dimensions={0} | all-to-all | bytes 131072 | tf_op jit(solution)/shard_map/all_to_all | solution.py:380
  61.3 0.8 %final_part.1 = f32[32,256]{1,0:T(8,128)} custom-call(f32[16,8,128]{2,1,0:T(8,128)S(1)} %all_to_all.11.x_ref), custom_call_target="tpu_custom_call" | custom-call | tf_op jit(solution)/shard_map/final_part/pallas_call | solution.py:343
  (3 shorter events, 0.0 us)
Async XLA Ops:
  4.3 31.6 %slice-start = ((s8[8388608]{0:T(1024)(128)(4,1)}), s8[4194304]{0:T(1024)(128)(4,1)S(1)}, s32[]{:S(2)}) async-start(s8[8388608]{0:T(1024)(128)(4,1)} %bitcast.1), calls=%async_computation.2 | async-start | bytes 8388608
  4.3 30.4 %copy-start = (f32[4,256,1024]{2,1,0:T(8,128)S(1)}, f32[4,256,1024]{2,1,0:T(8,128)}, u32[]{:S(2)}) copy-start(f32[4,256,1024]{2,1,0:T(8,128)} %w_ref.7) | copy-start | bytes 12582916
  4.4 30.4 %copy-start.1 = (f32[256,512]{1,0:T(8,128)S(1)}, f32[256,512]{1,0:T(8,128)}, u32[]{:S(2)}) copy-start(f32[256,512]{1,0:T(8,128)} %e_ref.3) | copy-start | bytes 1572868
  4.4 31.6 %slice-start.1 = ((s8[8388608]{0:T(1024)(128)(4,1)}), s8[4194304]{0:T(1024)(128)(4,1)S(1)}, s32[]{:S(2)}) async-start(s8[8388608]{0:T(1024)(128)(4,1)} %bitcast.1), calls=%async_computation.3 | async-start | bytes 8388608
  35.3 14.3 %collective-permute-start.3 = (f32[256,512]{1,0:T(8,128)S(1)}, f32[256,512]{1,0:T(8,128)S(1)}, u32[]{:S(2)}, u32[]{:S(2)}) collective-permute-start(f32[256,512]{1,0:T(8,128)S(1)} %far_part.1), channel_id=1, source_target_pairs={{0,8},{1,9},{2,10},{3,11},{4,12},{5,13},{6,14},{7,15},{8,0},{9,1},... | collective-permute-start | bytes 1572872 | tf_op jit(solution)/shard_map/ppermute | solution.py:353
  37.6 1.3 %collective-permute-start = (f32[64,256]{1,0:T(8,128)S(1)}, f32[64,256]{1,0:T(8,128)S(1)}, u32[]{:S(2)}, u32[]{:S(2)}) collective-permute-start(f32[64,256]{1,0:T(8,128)S(1)} %gram.1.c_ref), channel_id=1, source_target_pairs={{0,1},{1,0},{2,3},{3,2},{4,5},{5,4},{6,7},{7,6},{8,9},{9,8},{10,11... | collective-permute-start | bytes 196616 | tf_op jit(solution)/shard_map/ppermute | solution.py:353
  39.2 4.3 %collective-permute-start.1 = (f32[64,256]{1,0:T(8,128)S(1)}, f32[64,256]{1,0:T(8,128)S(1)}, u32[]{:S(2)}, u32[]{:S(2)}) collective-permute-start(f32[64,256]{1,0:T(8,128)S(1)} %join_part.2.c_ref), channel_id=1, source_target_pairs={{0,2},{1,3},{2,0},{3,1},{4,6},{5,7},{6,4},{7,5},{8,10},{9,11},{10,... | collective-permute-start | bytes 196616 | tf_op jit(solution)/shard_map/ppermute | solution.py:353
  43.7 5.8 %collective-permute-start.2 = (f32[64,256]{1,0:T(8,128)S(1)}, f32[64,256]{1,0:T(8,128)S(1)}, u32[]{:S(2)}, u32[]{:S(2)}) collective-permute-start(f32[64,256]{1,0:T(8,128)S(1)} %join_part.3.c_ref), channel_id=1, source_target_pairs={{0,4},{1,5},{2,6},{3,7},{4,0},{5,1},{6,2},{7,3},{8,12},{9,13},{10,... | collective-permute-start | bytes 196616 | tf_op jit(solution)/shard_map/ppermute | solution.py:353

commit v7 on v6

--- a/solution.py
+++ b/solution.py
@@ -221,11 +221,11 @@
 
 def fold(e, w, first):
     k = w.shape[0]
-    left = split(jnp.concatenate([e[:, :k], e[:, k:]], axis=0))
-    right = [w[:, at : at + k] for at in (first, first + 2 * k)]
-    both = mm3(left, split(jnp.concatenate(right, axis=1)), NN)
-    real = both[:k, :k] - both[k:, k:]
-    imag = both[:k, k:] + both[k:, :k]
+    a, b = e[:, :k], e[:, k:]
+    c, d = (w[:, at : at + k] for at in (first, first + 2 * k))
+    shared = mm3(split(a + b), split(c), NN)
+    real = shared - mm3(split(b), split(c + d), NN)
+    imag = shared + mm3(split(a), split(d - c), NN)
     return jnp.concatenate([real, imag], axis=1)
 
 

time: 62.2 us -> 62.1 us (level)
  transfers between devices with their start and end apart: 4 -> 4, of which waited for: 3 -> 3; matrix products, arithmetic and copies ran while one was open for 0% -> 0% of each run, Pallas kernels for 6% -> 5%
where the time goes in v7:
time: 62.1 us; the launch traced here: 62 us
  blocking collectives  41.2 us (66%)
  Pallas kernels  9.71 us (16%)
  waiting for transfers between devices  9.49 us (15%)
  starting transfers between devices  1.4 us (2%)
    all_to_all x1, blocking collectives, body(): lax.all_to_all(blocks, ('freq', 'trace'), split_axis=0, concat_axis=0, ti...  30.3 us
    all_to_all x1, blocking collectives, body(): lax.all_to_all(out, ('freq', 'trace'), 0, 0, axis_index_groups=groups, ti...  10.9 us
    ppermute x4, waiting for transfers between devices, from_partner(): lax.ppermute(block, axis, [(at, at ^ 1 << apart) for at in range(count)])  9.49 us
    pallas_call x1, Pallas kernels, trace_blocks(): pl.pallas_call(functools.partial(trace_kernel, scale), in_specs=[pl.Block...  4.32 us
    pallas_call x1, Pallas kernels, gram(): pl.pallas_call(gram_kernel, grid=(steps,), in_specs=[pl.BlockSpec((sender...  1.66 us
    ppermute x4, starting transfers between devices, from_partner(): lax.ppermute(block, axis, [(at, at ^ 1 << apart) for at in range(count)])  1.4 us
    pallas_call x3, Pallas kernels, own_part(): pl.pallas_call(own_kernel if e is None else own_fold_kernel, grid=(1,), i...  1.24 us
  transfers between devices with their start and end apart: 4, of which 3 were waited for; matrix products, arithmetic and copies ran while one was open for 0% of the time, Pallas kernels for 5%

profile of v7, /device:TPU:0, one launch (start us, length us, event | category | flops | bytes accessed | tf_op | source)
XLA Modules:
  0.0 62.0 jit_solution(3838484062054941894)
XLA Ops:
  0.0 4.3 %trace_blocks.1 = f32[8,16,16,128]{3,2,1,0:T(8,128)S(1)} custom-call(f32[2,256,2048]{2,1,0:T(8,128)} %x_hbm.1, f32[8,128,128]{2,1,0:T(8,128)} %constant.2.clone.table_hbm), custom_call_target="tpu_custom_call" | custom-call | tf_op jit(solution)/shard_map/trace_blocks/pallas_call | solution.py:132
  4.3 0.0 slice-start
  4.3 0.0 copy-start
  4.4 0.0 copy-start.1
  4.4 0.0 slice-start.1
  4.4 30.3 %all_to_all.10.values_ref.after_ref = f32[128,16,128]{2,1,0:T(8,128)S(1)} all-to-all(f32[128,16,128]{2,1,0:T(8,128)S(1)} %hold.3), channel_id=1, replica_groups=mesh['freq'=8,'trace'=16] {'freq','trace'}, dimensions={0} | all-to-all | bytes 2097152 | tf_op jit(solution)/shard_map/all_to_all | solution.py:362
  34.7 0.0 copy-done
  34.7 0.0 copy-done.1
  34.7 0.5 far_part.1
  35.2 0.6 %collective-permute-start.3 = (f32[256,512]{1,0:T(8,128)S(1)}, f32[256,512]{1,0:T(8,128)S(1)}, u32[]{:S(2)}, u32[]{:S(2)}) collective-permute-start(f32[256,512]{1,0:T(8,128)S(1)} %far_part.1), channel_id=1, source_target_pairs={{0,8},{1,9},{2,10},{3,11},{4,12},{5,13},{6,14},{7,15},{8,0},{9,1},... | collective-permute-start | bytes 1572872 | tf_op jit(solution)/shard_map/ppermute | solution.py:353
  35.9 0.0 slice-done
  35.9 0.0 slice-done.1
  35.9 1.7 %gram.1.c_ref = f32[64,256]{1,0:T(8,128)S(1)} custom-call(f32[128,16,128]{2,1,0:T(8,128)S(1)} %all_to_all.10.values_ref.after_ref, f32[256,16,512]{2,1,0:T(8,128)S(1)} %bitcast.2), custom_call_target="tpu_custom_call" | custom-call | tf_op jit(solution)/shard_map/gram/pallas_call | solution.py:207
  37.5 0.1 collective-permute-start
  37.6 0.3 own_part.2
  37.9 0.9 %collective-permute-done.c_ref = f32[64,256]{1,0:T(8,128)S(1)} collective-permute-done((f32[64,256]{1,0:T(8,128)S(1)}, f32[64,256]{1,0:T(8,128)S(1)}, u32[]{:S(2)}, u32[]{:S(2)}) %collective-permute-start) | collective-permute-done | bytes 65568 | tf_op jit(solution)/shard_map/ppermute | solution.py:353
  38.9 0.2 join_part.2.c_ref
  39.1 0.1 collective-permute-start.1
  39.2 0.6 %own_fold_part.1 = (f32[64,256]{1,0:T(8,128)S(1)}, bf16[256,512]{1,0:T(8,128)(2,1)S(1)}, bf16[256,512]{1,0:T(8,128)(2,1)S(1)}, bf16[256,512]{1,0:T(8,128)(2,1)S(1)}, bf16[256,512]{1,0:T(8,128)(2,1)S(1)}) custom-call(f32[64,256]{1,0:T(8,128)S(1)} %join_part.2.c_ref, f32[4,256,1024]{2,1,0:T(8,128)S(1)} %copy-done, f32[256,512]{1,0:T(8,128)S(1)} %copy-done.1, ...), custom_call_target="tpu_custom_call" | custom-call | flops 100000000 | bytes 1000000 | tf_op jit(solution)/shard_map/own_fold_part/pallas_call | solution.py:278
  39.8 3.6 %collective-permute-done.1.c_ref = f32[64,256]{1,0:T(8,128)S(1)} collective-permute-done((f32[64,256]{1,0:T(8,128)S(1)}, f32[64,256]{1,0:T(8,128)S(1)}, u32[]{:S(2)}, u32[]{:S(2)}) %collective-permute-start.1) | collective-permute-done | bytes 65568 | tf_op jit(solution)/shard_map/ppermute | solution.py:353
  43.4 0.2 join_part.3.c_ref
  43.6 0.6 collective-permute-start.2
  44.3 0.3 own_part.3
  44.5 5.0 %collective-permute-done.2.c_ref = f32[64,256]{1,0:T(8,128)S(1)} collective-permute-done((f32[64,256]{1,0:T(8,128)S(1)}, f32[64,256]{1,0:T(8,128)S(1)}, u32[]{:S(2)}, u32[]{:S(2)}) %collective-permute-start.2) | collective-permute-done | bytes 65568 | tf_op jit(solution)/shard_map/ppermute | solution.py:353
  49.5 0.0 collective-permute-done.3.far_ref
  49.5 0.8 %last_part.1 = f32[16,8,128]{2,1,0:T(8,128)S(1)} custom-call(f32[64,256]{1,0:T(8,128)S(1)} %get-tuple-element.22.own_ref, f32[64,256]{1,0:T(8,128)S(1)} %collective-permute-done.2.c_ref, bf16[256,512]{1,0:T(8,128)(2,1)S(1)} %get-tuple-element.23.high_ref, bf16[256,512]{1,0:T(8,128)(2,1)S(1)} %get-tuple-element.24.low_ref, ...), custom_call_target="tpu_custom_call" | custom-call | tf_op jit(solution)/shard_map/last_part/pallas_call | solution.py:324
  50.3 10.9 %all_to_all.11.x_ref = f32[16,8,128]{2,1,0:T(8,128)S(1)} all-to-all(f32[16,8,128]{2,1,0:T(8,128)S(1)} %last_part.1), channel_id=1, replica_groups={{0,8,16,24,32,40,48,56,64,72,80,88,96,104,112,120},{1,9,17,25,33,41,49,..., dimensions={0} | all-to-all | bytes 131072 | tf_op jit(solution)/shard_map/all_to_all | solution.py:380
  61.2 0.8 %final_part.1 = f32[32,256]{1,0:T(8,128)} custom-call(f32[16,8,128]{2,1,0:T(8,128)S(1)} %all_to_all.11.x_ref), custom_call_target="tpu_custom_call" | custom-call | tf_op jit(solution)/shard_map/final_part/pallas_call | solution.py:343
  (3 shorter events, 0.0 us)
Async XLA Ops:
  4.3 31.5 %slice-start = ((s8[8388608]{0:T(1024)(128)(4,1)}), s8[4194304]{0:T(1024)(128)(4,1)S(1)}, s32[]{:S(2)}) async-start(s8[8388608]{0:T(1024)(128)(4,1)} %bitcast.1), calls=%async_computation.2 | async-start | bytes 8388608
  4.3 30.4 %copy-start = (f32[4,256,1024]{2,1,0:T(8,128)S(1)}, f32[4,256,1024]{2,1,0:T(8,128)}, u32[]{:S(2)}) copy-start(f32[4,256,1024]{2,1,0:T(8,128)} %w_ref.7) | copy-start | bytes 12582916
  4.4 30.4 %copy-start.1 = (f32[256,512]{1,0:T(8,128)S(1)}, f32[256,512]{1,0:T(8,128)}, u32[]{:S(2)}) copy-start(f32[256,512]{1,0:T(8,128)} %e_ref.3) | copy-start | bytes 1572868
  4.4 31.5 %slice-start.1 = ((s8[8388608]{0:T(1024)(128)(4,1)}), s8[4194304]{0:T(1024)(128)(4,1)S(1)}, s32[]{:S(2)}) async-start(s8[8388608]{0:T(1024)(128)(4,1)} %bitcast.1), calls=%async_computation.3 | async-start | bytes 8388608
  35.2 14.3 %collective-permute-start.3 = (f32[256,512]{1,0:T(8,128)S(1)}, f32[256,512]{1,0:T(8,128)S(1)}, u32[]{:S(2)}, u32[]{:S(2)}) collective-permute-start(f32[256,512]{1,0:T(8,128)S(1)} %far_part.1), channel_id=1, source_target_pairs={{0,8},{1,9},{2,10},{3,11},{4,12},{5,13},{6,14},{7,15},{8,0},{9,1},... | collective-permute-start | bytes 1572872 | tf_op jit(solution)/shard_map/ppermute | solution.py:353
  37.5 1.3 %collective-permute-start = (f32[64,256]{1,0:T(8,128)S(1)}, f32[64,256]{1,0:T(8,128)S(1)}, u32[]{:S(2)}, u32[]{:S(2)}) collective-permute-start(f32[64,256]{1,0:T(8,128)S(1)} %gram.1.c_ref), channel_id=1, source_target_pairs={{0,1},{1,0},{2,3},{3,2},{4,5},{5,4},{6,7},{7,6},{8,9},{9,8},{10,11... | collective-permute-start | bytes 196616 | tf_op jit(solution)/shard_map/ppermute | solution.py:353
  39.1 4.3 %collective-permute-start.1 = (f32[64,256]{1,0:T(8,128)S(1)}, f32[64,256]{1,0:T(8,128)S(1)}, u32[]{:S(2)}, u32[]{:S(2)}) collective-permute-start(f32[64,256]{1,0:T(8,128)S(1)} %join_part.2.c_ref), channel_id=1, source_target_pairs={{0,2},{1,3},{2,0},{3,1},{4,6},{5,7},{6,4},{7,5},{8,10},{9,11},{10,... | collective-permute-start | bytes 196616 | tf_op jit(solution)/shard_map/ppermute | solution.py:353
  43.6 5.8 %collective-permute-start.2 = (f32[64,256]{1,0:T(8,128)S(1)}, f32[64,256]{1,0:T(8,128)S(1)}, u32[]{:S(2)}, u32[]{:S(2)}) collective-permute-start(f32[64,256]{1,0:T(8,128)S(1)} %join_part.3.c_ref), channel_id=1, source_target_pairs={{0,4},{1,5},{2,6},{3,7},{4,0},{5,1},{6,2},{7,3},{8,12},{9,13},{10,... | collective-permute-start | bytes 196616 | tf_op jit(solution)/shard_map/ppermute | solution.py:353
